TPU v7x, 1024 devices: a whole 4x8x16 slice. The times are simulated.
1024 devices in a mesh: band: 32 (over z_lo, y), ga: 32 (over z_hi, x, core).
Axes of the slice: x: 4, y: 8, z: 16 (z_hi: 4, z_lo: 4; z = z_hi * 4 + z_lo), core: 2. Of those that a mesh axis runs over, the one named last changes fastest.
Arguments:
- valence: bfloat16 [32, 2, 128, 128, 128], P('band', None, 'ga'), may hold values from -6 to 6
- conduction: bfloat16 [192, 128, 128, 128], P('band', 'ga'), may hold values from -6 to 6
- owners: int32 [2], replicated, may hold values from 0 to 31
- val_energy: float32 [2], replicated, may hold values from -8 to -4
- cond_energy: float32 [192], P('band'), may hold values from 0.5 to 20
- gvec_index: int32 [10240], P('ga'), may hold values from 0 to 8191, as said below
Outputs:
- chi_panel: float32 [10240, 4096], P('band', 'ga')
Inputs may be any that keep to these rules, and one draw needn't show every extreme that they name: owners[k] is the band group whose slot k holds valence band k. `gvec_index`: within each block j of 320 entries the values are distinct; value a 128 + b * 64 + c names x-frequency index a, y-frequency index j * 2 + b, z-frequency index c.
All inputs are finite; a program needn't handle non-finite values.
Results may differ from a plain program's by a relative error of at most 0.0048.
Values may be sent and summed in bfloat16 or wider, within the bound.
A program may use at most 32 MiB of HBM per device.

v0:
```python
import math

import jax
import jax.numpy as jnp
from jax import lax
from jax.sharding import PartitionSpec as P

NGRID = 128
KB = 64
NV = 2
PANEL_DEV = 128


highest = lax.Precision.HIGHEST


def spread_2(block, axis, holder):
    block = jnp.where(lax.axis_index(axis) == holder, block, jnp.zeros_like(block))
    return lax.psum(block, axis)


def dft_tables(grid_count, freq_count):
    grid_points = jnp.arange(grid_count, dtype=jnp.int32)
    shifted = jnp.arange(freq_count, dtype=jnp.int32) - freq_count // 2
    phase_index = grid_points[:, None] * shifted[None, :] % grid_count
    angles = phase_index.astype(jnp.float32) * (2.0 * math.pi / grid_count)
    scale_factor = 1.0 / math.sqrt(grid_count)
    return (jnp.cos(angles) * scale_factor, -jnp.sin(angles) * scale_factor)


def front_half(fields, cosine_table, sine_table, freq_count):
    both_tables = jnp.concatenate([cosine_table, sine_table], axis=1)
    zpart = jnp.einsum("fxyz,zq->fxyq", fields, both_tables, precision=highest)
    real_z, imag_z = (zpart[..., :freq_count], zpart[..., freq_count:])
    real_y = jnp.einsum("fxyk,yq->fxqk", real_z, cosine_table, precision=highest) - jnp.einsum(
        "fxyk,yq->fxqk", imag_z, sine_table, precision=highest
    )
    imag_y = jnp.einsum("fxyk,yq->fxqk", imag_z, cosine_table, precision=highest) + jnp.einsum(
        "fxyk,yq->fxqk", real_z, sine_table, precision=highest
    )
    return jnp.concatenate([real_y, imag_y], axis=-1)


def back_half(arrived, cosine_table, sine_table, freq_count):
    real_y, imag_y = (arrived[..., :freq_count], arrived[..., freq_count:])
    real_x = jnp.einsum("fxjk,xq->fqjk", real_y, cosine_table, precision=highest) - jnp.einsum(
        "fxjk,xq->fqjk", imag_y, sine_table, precision=highest
    )
    imag_x = jnp.einsum("fxjk,xq->fqjk", imag_y, cosine_table, precision=highest) + jnp.einsum(
        "fxjk,xq->fqjk", real_y, sine_table, precision=highest
    )
    return jnp.concatenate([real_x, imag_x], axis=-1)


def per_device(valence, conduction, owners, val_energy, cond_energy, gvec_index):
    cosine_table, sine_table = dft_tables(NGRID, KB)
    local_val = valence[0]
    waves = conduction.astype(jnp.float32)
    spectra_list = []
    for band_slot in range(NV):
        val_field = spread_2(local_val[band_slot], "band", owners[band_slot]).astype(jnp.float32)
        fields = waves * val_field[None]
        partial_value = front_half(fields, cosine_table, sine_table, KB)
        arrived = lax.all_to_all(partial_value, "ga", split_axis=2, concat_axis=1, tiled=True)
        spectra_list.append(back_half(arrived, cosine_table, sine_table, KB))
    spectra = jnp.concatenate(spectra_list, axis=0)
    field_count = spectra.shape[0]
    kyd_local = spectra.shape[2]
    arranged = (
        spectra.reshape(field_count, KB, kyd_local, 2, KB)
        .transpose(0, 3, 1, 2, 4)
        .reshape(field_count, 2, -1)
    )
    picked = arranged[:, :, gvec_index]
    coeffs = picked.reshape(field_count * 2, -1).astype(jnp.bfloat16)
    weights = 1.0 / (val_energy[:, None] - cond_energy[None, :])
    col_weights = jnp.repeat(weights.reshape(-1), 2)
    weighted = (coeffs[:, :PANEL_DEV].astype(jnp.float32) * col_weights[:, None]).astype(
        jnp.bfloat16
    )
    gathered = lax.all_gather(coeffs, "ga", axis=1, tiled=True)
    contract = (((0,), (0,)), ((), ()))
    return lax.psum_scatter(
        lax.dot_general(gathered, weighted, contract, preferred_element_type=jnp.float32),
        "band",
        scatter_dimension=0,
        tiled=True,
    )


def solution(mesh):
    in_specs = (
        P("band", None, "ga", None, None),
        P("band", "ga", None, None),
        P(),
        P(),
        P("band"),
        P("ga"),
    )
    out_specs = P("band", "ga")
    return jax.shard_map(
        per_device, mesh=mesh, in_specs=in_specs, out_specs=out_specs, check_vma=False
    )
```

profile of v0, /device:TPU:2, one launch (start us, length us, event | category | flops | bytes accessed | tf_op | source)
XLA Modules:
  0.0 695.9 jit_solution(15677362584682349023)
XLA Ops:
  6.5 1.4 fusion.143
  9.2 1.7 select_bitcast_fusion.1
  10.9 0.2 cosine_multiply_fusion
  11.1 328.3 %all-reduce.3.cloned.1.call-done = (bf16[4,128,128]{2,1,0:T(8,128)(2,1)}, bf16[4,128,128]{2,1,0:T(8,128)(2,1)}) async-done(((bf16[4,128,128]{2,1,0:T(8,128)(2,1)}, bf16[4,128,128]{2,1,0:T(8,128)(2,1)}), (bf16[4,128,128]{2,1,0:T(8,128)(2,1)}, bf16[4,128,128]{2,1,0:T(8,128)(2,1)})) %all-reduce.3.cloned.1.call-update) | async-done | bytes 262160 | tf_op jit(solution)/shard_map/psum | solution.py:19
  339.4 0.9 convert_element_type.60
  340.3 1.7 fusion
  342.0 2.5 fusion.30
  344.5 2.5 fusion.34
  347.1 2.6 fusion.4
  349.6 2.6 fusion.5
  352.2 0.3 pad_maximum_fusion
  352.5 1.4 copy.27
  353.9 13.8 %all-to-all-start = ((f32[6,4,64,128]{3,1,0,2:T(4,128)}), f32[6,4,64,128]{3,1,0,2:T(4,128)S(1)}, u32[]{:S(2)}, u32[]{:S(2)}) async-start(f32[6,4,64,128]{3,1,0,2:T(4,128)} %copy.27), calls=%async_computation | async-start | bytes 1572864 | tf_op jit(solution)/shard_map/all_to_all | solution.py:64
  367.8 1.7 fusion.1
  369.5 2.5 fusion.18
  372.0 2.5 fusion.22
  374.6 2.6 fusion.2
  377.1 2.6 fusion.3
  379.7 0.3 pad_maximum_fusion.1
  380.0 1.4 copy.31
  381.4 14.1 %all-to-all-done = f32[6,4,64,128]{3,1,0,2:T(4,128)S(1)} async-done(((f32[6,4,64,128]{3,1,0,2:T(4,128)}), f32[6,4,64,128]{3,1,0,2:T(4,128)S(1)}, u32[]{:S(2)}, u32[]{:S(2)}) %all-to-all-start) | async-done | bytes 786464 | tf_op jit(solution)/shard_map/all_to_all | solution.py:64
  395.5 10.0 %all-to-all-start.1 = ((f32[6,4,64,128]{3,1,0,2:T(4,128)}), f32[6,4,64,128]{3,1,0,2:T(4,128)S(1)}, u32[]{:S(2)}, u32[]{:S(2)}) async-start(f32[6,4,64,128]{3,1,0,2:T(4,128)} %copy.31), calls=%async_computation.1 | async-start | bytes 1572864 | tf_op jit(solution)/shard_map/all_to_all | solution.py:64
  405.5 0.3 reduce-scatter.2.cloned.1.call-start
  405.8 0.1 subtract_divide_fusion
  405.9 0.1 div.8
  406.0 0.1 broadcast_in_dim.5
  406.1 0.1 mul.230
  406.2 0.2 copy.28
  406.4 0.7 fusion.27
  407.1 0.8 fusion.25
  407.9 32.9 %all-to-all-done.1 = f32[6,4,64,128]{3,1,0,2:T(4,128)S(1)} async-done(((f32[6,4,64,128]{3,1,0,2:T(4,128)}), f32[6,4,64,128]{3,1,0,2:T(4,128)S(1)}, u32[]{:S(2)}, u32[]{:S(2)}) %all-to-all-start.1) | async-done | bytes 786464 | tf_op jit(solution)/shard_map/all_to_all | solution.py:64
  440.9 0.2 copy.32
  441.0 0.7 fusion.15
  441.8 0.8 fusion.13
  442.6 0.8 fusion.9
  443.4 0.7 fusion.8
  444.2 0.8 fusion.7
  445.0 0.7 fusion.6
  445.7 0.2 maximum_maximum_fusion
  446.0 0.3 reshape.33
  446.3 6.9 copy.42
  453.2 3.2 gather_fusion
  456.5 0.1 copy.37
  456.7 48.7 %all-gather = bf16[32,320,24]{1,2,0:T(8,128)(2,1)S(1)} all-gather(bf16[1,320,24]{1,2,0:T(8,128)(2,1)S(1)} %bitcast.103), channel_id=1, replica_groups=mesh['band'=32,'ga'=32] {'ga'}, dimensions={0}, use_global_device_ids=true | all-gather | bytes 506880 | tf_op jit(solution)/shard_map/all_gather | solution.py:81
  505.4 0.1 copy.38
  505.4 0.6 reshape.45
  506.0 3.2 fusion.58
  509.3 179.7 %reduce-scatter.2.cloned.1.call-done = f32[320,128]{1,0:T(8,128)} async-done(((f32[10240,128]{1,0:T(8,128)}), f32[320,128]{1,0:T(8,128)}) %reduce-scatter.2.cloned.1.call-update) | async-done | bytes 163856 | tf_op jit(solution)/shard_map/reduce_scatter | solution.py:83
  (18 shorter events, 0.1 us)
Async XLA Ops:
  6.5 333.8 %copy-start = (bf16[6,4,128,128]{3,2,1,0:T(8,128)(2,1)S(1)}, bf16[6,4,128,128]{3,2,1,0:T(8,128)(2,1)}, u32[]{:S(2)}) copy-start(bf16[6,4,128,128]{3,2,1,0:T(8,128)(2,1)} %param.7) | copy-start | bytes 2359300
  6.5 332.9 %all-reduce.3.cloned.1.call-start = ((), (), s32[]{:S(2)}) async-start(), calls=%async_computation.4 | async-start | bytes 524288 | tf_op jit(solution)/shard_map/psum | solution.py:19
  352.5 15.3 %copy-start.1 = (bf16[4,128,128]{2,1,0:T(8,128)(2,1)S(1)}, bf16[4,128,128]{2,1,0:T(8,128)(2,1)}, u32[]{:S(2)}) copy-start(bf16[4,128,128]{2,1,0:T(8,128)(2,1)} %get-tuple-element.5) | copy-start | bytes 393220
  353.9 41.6 %all-to-all-start = ((f32[6,4,64,128]{3,1,0,2:T(4,128)}), f32[6,4,64,128]{3,1,0,2:T(4,128)S(1)}, u32[]{:S(2)}, u32[]{:S(2)}) async-start(f32[6,4,64,128]{3,1,0,2:T(4,128)} %copy.27), calls=%async_computation | async-start | bytes 1572864 | tf_op jit(solution)/shard_map/all_to_all | solution.py:64
  379.9 25.9 %copy-start.3 = (f32[6]{0:T(128)S(1)}, f32[6]{0:T(128)}, u32[]{:S(2)}) copy-start(f32[6]{0:T(128)} %param.10) | copy-start | bytes 76
  379.9 25.9 %copy-start.4 = (f32[2]{0:T(128)S(1)}, f32[2]{0:T(128)}, u32[]{:S(2)}) copy-start(f32[2]{0:T(128)} %param.9) | copy-start | bytes 28
  380.0 26.2 %copy-start.2 = (s32[320]{0:T(512)S(1)}, s32[320]{0:T(512)}, u32[]{:S(2)}) copy-start(s32[320]{0:T(512)} %param.11) | copy-start | bytes 3844
  395.5 45.3 %all-to-all-start.1 = ((f32[6,4,64,128]{3,1,0,2:T(4,128)}), f32[6,4,64,128]{3,1,0,2:T(4,128)S(1)}, u32[]{:S(2)}, u32[]{:S(2)}) async-start(f32[6,4,64,128]{3,1,0,2:T(4,128)} %copy.31), calls=%async_computation.1 | async-start | bytes 1572864 | tf_op jit(solution)/shard_map/all_to_all | solution.py:64
  405.5 283.5 %reduce-scatter.2.cloned.1.call-start = ((), (), s32[]{:S(2)}) async-start(), calls=%async_computation.3 | async-start | bytes 5406720 | tf_op jit(solution)/shard_map/reduce_scatter | solution.py:83
Sparse Core Ops, SparseCore 0:
  11.0 328.3 all-reduce.2
  509.4 179.5 reduce-scatter.1
where the time goes:
time: 696 us
  waiting for transfers between devices  555 us (80%)
  blocking collectives  48.7 us (7%)
  matrix products  33.1 us (5%)
  starting transfers between devices  24.1 us (3%)
  local copies, waits for them, and re-layouts  16.2 us (2%)
  between operations  15 us (2%)
    psum x1, waiting for transfers between devices, spread_2(): return lax.psum(block, axis)  328 us
    reduce_scatter x1, waiting for transfers between devices, per_device(): lax.psum_scatter(lax.dot_general(gathered, weighted, contract, preferred_...  180 us
    all_gather x1, blocking collectives, per_device(): gathered = lax.all_gather(coeffs, 'ga', axis=1, tiled=True)  48.7 us
    all_to_all x2, waiting for transfers between devices, per_device(): lax.all_to_all(partial_value, 'ga', split_axis=2, concat_axis=1, tiled=True)  47.1 us
    all_to_all x2, starting transfers between devices, per_device(): lax.all_to_all(partial_value, 'ga', split_axis=2, concat_axis=1, tiled=True)  23.8 us
  transfers between devices with their start and end apart: 4, of which 4 were waited for; matrix products, arithmetic and copies ran while one was open for 2% of the time, Pallas kernels for 0%

commit v1 on v0

v1 whole, which is shorter than its diff:
```python
import math

import jax
import jax.numpy as jnp
import numpy as np
from jax import lax
from jax.experimental import pallas as pl
from jax.experimental.pallas import tpu as pltpu
from jax.sharding import PartitionSpec as P

NGRID = 128
KB = 64
NV = 2
NC = 6
NF = NV * NC
NGD = 320
PANEL = 128
NB = 32
NGA = 32

F32 = jnp.float32
BF16 = jnp.bfloat16
MESH = pl.DeviceIdType.MESH
VMEM = pl.BlockSpec(memory_space=pltpu.VMEM)
SMEM = pl.BlockSpec(memory_space=pltpu.SMEM)


def split_table(table, terms):
    parts = []
    rest = table.astype(np.float32)
    for _ in range(terms):
        part = rest.astype(jnp.bfloat16)
        parts.append(part)
        rest = rest - part.astype(np.float32)
    return parts


def tables():
    n = np.arange(NGRID)[:, None]
    m = np.arange(KB)[None, :] - KB // 2
    angle = ((n * m) % NGRID).astype(np.float64) * (2.0 * math.pi / NGRID)
    scale = 1.0 / math.sqrt(NGRID)
    c = np.cos(angle) * scale
    s = -np.sin(angle) * scale
    zh, zl = split_table(np.concatenate([c, s, -s, c], axis=1), 2)
    ztab = np.stack([np.concatenate([zh, zh], axis=0), np.concatenate([zl, zl], axis=0)])
    yh, yl = split_table(np.concatenate([c.T, s.T], axis=1), 2)
    ytab = np.concatenate([yh, yl], axis=0)
    own = np.concatenate([c.reshape(NGA, 4, KB), s.reshape(NGA, 4, KB)], axis=1)
    parts = split_table(own, 3)
    xtab = np.concatenate(parts + [np.zeros_like(parts[0])], axis=1)
    return ztab, ytab, xtab


def spread_kernel(own_ref, val_ref, gv_ref, out_ref, gva_ref, masked, recv, ss, sr, gs, gr, vs, vr):
    b = lax.axis_index("band")
    a = lax.axis_index("ga")
    barrier = pltpu.get_barrier_semaphore()

    def greet(d, carry):
        pl.semaphore_signal(barrier, 1, device_id=(lax.rem(b + d, NB), a), device_id_type=MESH)
        pl.semaphore_signal(barrier, 1, device_id=(b, lax.rem(a + d, NGA)), device_id_type=MESH)
        return carry

    lax.fori_loop(1, NB, greet, 0)
    half = NB // NV
    for k in range(NV):
        flag = jnp.where(own_ref[k] == b, 1.0, 0.0).astype(F32)
        block = val_ref[k * half : (k + 1) * half].astype(F32)
        masked[k * half : (k + 1) * half] = (block * flag).astype(BF16)
    gva_ref[a] = gv_ref[...]
    pl.semaphore_wait(barrier, 2 * (NB - 1))

    def piece(p):
        return pltpu.make_async_remote_copy(
            masked.at[p], recv.at[b], ss.at[p], sr.at[b], device_id=(p, a), device_id_type=MESH
        )

    def piece_in(p):
        return pltpu.make_async_remote_copy(
            masked.at[p], recv.at[p], ss.at[p], sr.at[p], device_id=(p, a), device_id_type=MESH
        )

    def whole(p):
        return pltpu.make_async_remote_copy(
            out_ref.at[b], out_ref.at[b], gs.at[p], gr.at[b], device_id=(p, a), device_id_type=MESH
        )

    def whole_in(p):
        return pltpu.make_async_remote_copy(
            out_ref.at[b], out_ref.at[p], gs.at[p], gr.at[p], device_id=(p, a), device_id_type=MESH
        )

    def gvec(q):
        return pltpu.make_async_remote_copy(
            gv_ref, gva_ref.at[a], vs.at[q], vr.at[a], device_id=(b, q), device_id_type=MESH
        )

    def gvec_in(q):
        return pltpu.make_async_remote_copy(
            gv_ref, gva_ref.at[q], vs.at[q], vr.at[q], device_id=(b, q), device_id_type=MESH
        )

    def over_band(fn):
        lax.fori_loop(1, NB, lambda d, carry: (fn(lax.rem(b + d, NB)), carry)[1], 0)

    def over_ga(fn):
        lax.fori_loop(1, NGA, lambda d, carry: (fn(lax.rem(a + d, NGA)), carry)[1], 0)

    over_band(lambda p: piece(p).start())
    over_ga(lambda q: gvec(q).start())

    def add(d, total):
        p = lax.rem(b + NB - d, NB)
        piece_in(p).wait_recv()
        return total + recv[p].astype(F32)

    total = lax.fori_loop(1, NB, add, masked[b].astype(F32))
    out_ref[b] = total.astype(BF16)
    over_band(lambda p: whole(p).start())
    over_ga(lambda q: gvec_in(q).wait_recv())
    over_band(lambda p: whole_in(p).wait_recv())
    over_band(lambda p: piece(p).wait_send())
    over_band(lambda p: whole(p).wait_send())
    over_ga(lambda q: gvec(q).wait_send())


def dot(x, y):
    return jnp.dot(x, y, preferred_element_type=F32)


def split(x):
    high = x.astype(BF16)
    return high, (x - high.astype(F32)).astype(BF16)


def compute_kernel(me_ref, cond_ref, val_ref, gva_ref, zt_ref, yt_ref, xt_ref, p_ref, y_scr):
    zeros = jnp.zeros((4 * KB, 128), F32)
    for xl in range(4):
        y_scr[(xl * 16 + NF) * KB : (xl + 1) * 16 * KB, :] = zeros

    def field(f, carry):
        c = lax.div(f, NV)
        k = lax.rem(f, NV)
        pair = (cond_ref[c].astype(F32) * val_ref[k].astype(F32)).reshape(4 * NGRID, NGRID)
        hl = jnp.concatenate(split(pair), axis=1)
        z = dot(hl, zt_ref[0]) + dot(hl, zt_ref[1])
        for xl in range(4):
            part = z[xl * NGRID : (xl + 1) * NGRID]
            zh, zl = split(jnp.concatenate([part[:, :128], part[:, 128:]], axis=0))
            both = dot(yt_ref[...], zh)
            out = both[:KB] + (both[KB:] + dot(yt_ref[0:KB, :], zl))
            row = pl.multiple_of((xl * 16 + f) * KB, KB)
            y_scr[pl.ds(row, KB), :] = out
        return carry

    lax.fori_loop(0, NF, field, 0)
    xt = xt_ref[me_ref[0]]
    lane = lax.broadcasted_iota(jnp.int32, (64, 128), 1) < KB
    cell = lax.broadcasted_iota(jnp.int32, (128, NGD), 0)
    xcell = lax.broadcasted_iota(jnp.int32, (KB, NGD), 0)

    def block(j, carry):
        y0 = y_scr[pl.ds(2 * j, 64, stride=KB), :]
        y1 = y_scr[pl.ds(2 * j + 1, 64, stride=KB), :]
        ur = jnp.where(lane, y0, pltpu.roll(y1, KB, 1))
        ui = jnp.where(lane, pltpu.roll(y0, KB, 1), y1)
        hl = jnp.concatenate(split(jnp.concatenate([ur, ui], axis=0)), axis=1)
        v = gva_ref[j]
        hot = jnp.where(cell == (v & 127), 1.0, 0.0).astype(BF16)
        xhot = jnp.where(xcell == (v >> 7), 1.0, 0.0).astype(BF16)
        sel = dot(hl, jnp.concatenate([hot, hot], axis=0))
        e3 = dot(xt, xhot)
        e = e3[0:8] + (e3[8:16] + e3[16:24])
        re = jnp.zeros((16, NGD), F32)
        im = jnp.zeros((16, NGD), F32)
        for xl in range(4):
            sr = sel[xl * 16 : (xl + 1) * 16]
            si = sel[64 + xl * 16 : 64 + (xl + 1) * 16]
            er = e[xl : xl + 1]
            ei = e[4 + xl : 5 + xl]
            re = re + (sr * er - si * ei)
            im = im + (si * er + sr * ei)
        zh = lax.div(j, 8)
        x = lax.rem(lax.div(j, 2), 4)
        c = lax.rem(j, 2)
        p_ref[c, x, zh] = jnp.concatenate([re[:NF], im[:NF]], axis=0)
        return carry

    lax.fori_loop(0, NGA, block, 0)


def exchange_kernel(
    p_ref, w_ref, r_ref, wo_ref, c_rcv, s1, x_rcv, s2, z_rcv, pack, t_buf, w_buf,
    cs, cr, xs, xr, zs, zr, ts, tr, ps, pr, xas, xar, cas, car,
):
    b = lax.axis_index("band")
    a = lax.axis_index("ga")
    zl, y = lax.div(b, 8), lax.rem(b, 8)
    zh, x, c = lax.div(a, 8), lax.rem(lax.div(a, 2), 4), lax.rem(a, 2)
    e = lax.rem(a, 8)
    other = a + 1 - 2 * c
    barrier = pltpu.get_barrier_semaphore()

    def copy(src, dst, send, recv, where):
        return pltpu.make_async_remote_copy(
            src, dst, send, recv, device_id=where, device_id_type=MESH
        )

    def at_x(xx):
        return (b, zh * 8 + xx * 2 + c)

    def at_z(zz):
        return (b, zz * 8 + x * 2 + c)

    def greet(band, ga):
        pl.semaphore_signal(barrier, 1, device_id=(band, ga), device_id_type=MESH)

    greet(b, other)
    for d in range(1, 4):
        greet(*at_x(lax.rem(x + d, 4)))
        greet(*at_z(lax.rem(zh + d, 4)))
    for s in range(4):
        source = s * 8 + e

        @pl.when(jnp.logical_or(source != b, a != b))
        def _():
            greet(source, b)

    def greet_band(d, carry):
        greet(lax.rem(b + d, NB), a)
        return carry

    lax.fori_loop(1, NB, greet_band, 0)
    pl.semaphore_wait(barrier, 38 + 4 - jnp.where(a == b, 1, 0))

    order = [lax.rem(x + d, 4) for d in (1, 2, 3)] + [x]
    core = [copy(p_ref.at[1 - c, xx], c_rcv.at[xx], cs.at[xx], cr.at[xx], (b, other)) for xx in order]
    for op in core:
        op.start()
    x_ops = []
    for op, xx in zip(core, order):
        op.wait_recv()
        s1[xx] = p_ref[c, xx] + c_rcv[xx]
        if len(x_ops) < 3:
            go = copy(s1.at[xx], x_rcv.at[x], xs.at[xx], xr.at[x], at_x(xx))
            go.start()
            x_ops.append(go)
    for xx in order[:3]:
        copy(s1.at[xx], x_rcv.at[xx], xs.at[xx], xr.at[xx], at_x(xx)).wait_recv()
    z_order = [lax.rem(zh + d, 4) for d in (2, 1, 3)] + [zh]
    z_ops = []
    for zz in z_order:
        s2[zz] = (s1[x, zz] + x_rcv[order[0], zz]) + (x_rcv[order[1], zz] + x_rcv[order[2], zz])
        if len(z_ops) < 3:
            go = copy(s2.at[zz], z_rcv.at[zh], zs.at[zz], zr.at[zh], at_z(zz))
            go.start()
            z_ops.append(go)
    for zz in z_order[:3]:
        copy(s2.at[zz], z_rcv.at[zz], zs.at[zz], zr.at[zz], at_z(zz)).wait_recv()
    total = (s2[zh] + z_rcv[z_order[0]]) + (z_rcv[z_order[1]] + z_rcv[z_order[2]])
    coeffs = total.astype(BF16).astype(F32)
    pack[0:24, :] = coeffs[:, 0:128]
    pack[24:48, :] = coeffs[:, 128:256]
    pack[48:64, 0:64] = coeffs[0:16, 256:320]
    pack[48:56, 64:128] = coeffs[16:24, 256:320]
    pack[56:64, 64:128] = jnp.zeros((8, 64), F32)
    t_buf[...] = pack[...].astype(BF16)
    for d in (2, 1, 3, 0):
        zz = lax.rem(zh + d, 4)
        target = zz * 8 + y
        stays = jnp.logical_and(a == b, target == a)

        @pl.when(jnp.logical_not(stays))
        def _():
            copy(t_buf, r_ref.at[y, zl], ts.at[zz], tr.at[zl], (a, target)).start()

        @pl.when(stays)
        def _():
            pltpu.make_async_copy(t_buf, r_ref.at[y, zl], tr.at[zl]).start()

    weighted = jnp.concatenate([coeffs[:, :PANEL] * w_ref[...], jnp.zeros((8, PANEL), F32)], axis=0)
    w_buf[...] = weighted.astype(BF16)
    wo_ref[b] = weighted.astype(BF16)

    def panel(p):
        return copy(w_buf, wo_ref.at[b], ps.at[p], pr.at[b], (p, a))

    def panel_in(p):
        return copy(w_buf, wo_ref.at[p], ps.at[p], pr.at[p], (p, a))

    def over_band(fn):
        lax.fori_loop(1, NB, lambda d, carry: (fn(lax.rem(b + d, NB)), carry)[1], 0)

    over_band(lambda p: panel(p).start())
    def along_x(ee, src_x, xx, s):
        return copy(r_ref.at[ee, s], r_ref.at[ee, s], xas.at[xx, s], xar.at[src_x, s], at_x(xx))

    def along_core(ee, s):
        return copy(r_ref.at[ee, s], r_ref.at[ee, s], cas.at[ee, s], car.at[ee, s], (b, other))

    for s in range(4):
        pltpu.make_async_copy(t_buf, r_ref.at[e, s], tr.at[s]).wait()
        for xx in order[:3]:
            along_x(e, x, xx, s).start()
        along_core(e, s).start()
    for s in range(4):
        for xx in order[:3]:
            ee = xx * 2 + c
            along_x(ee, xx, xx, s).wait_recv()
            along_core(ee, s).start()
    over_band(lambda p: panel_in(p).wait_recv())
    for s in range(4):
        for xx in order:
            along_core(xx * 2 + 1 - c, s).wait_recv()
    for op in core + x_ops + z_ops:
        op.wait_send()
    for d in range(4):
        zz = lax.rem(zh + d, 4)
        target = zz * 8 + y

        @pl.when(jnp.logical_not(jnp.logical_and(a == b, target == a)))
        def _():
            copy(t_buf, r_ref.at[y, zl], ts.at[zz], tr.at[zl], (a, target)).wait_send()

    over_band(lambda p: panel(p).wait_send())
    for s in range(4):
        for xx in order[:3]:
            along_x(e, x, xx, s).wait_send()
        for xx in order:
            along_core(xx * 2 + c, s).wait_send()


def chi_kernel(r_ref, wo_ref, out_ref, left, right):
    def place(s, carry):
        ee = lax.div(s, 4)
        zl = lax.rem(s, 4)
        block = r_ref[ee, zl].astype(F32)
        row = pl.multiple_of(s * 24, 8)
        left[pl.ds(row, 24), 0:128] = block[0:24]
        left[pl.ds(row, 24), 128:256] = block[24:48]
        left[pl.ds(row, 16), 256:320] = block[48:64, 0:64]
        left[pl.ds(row + 16, 8), 256:320] = block[48:56, 64:128]
        right[pl.ds(row, 24), :] = wo_ref[zl * 8 + ee].astype(F32)[0:24]
        return carry

    lax.fori_loop(0, NB, place, 0)
    out_ref[...] = lax.dot_general(
        left[...].astype(BF16),
        right[...].astype(BF16),
        (((0,), (0,)), ((), ())),
        preferred_element_type=F32,
    )


def per_device(valence, conduction, owners, val_energy, cond_energy, gvec_index, ztab, ytab, xtab):
    dma = pltpu.SemaphoreType.DMA
    piece = (NB, 32, 128)
    fields, gvecs = pl.pallas_call(
        spread_kernel,
        out_shape=(
            jax.ShapeDtypeStruct(piece, BF16),
            jax.ShapeDtypeStruct((NGA, 1, NGD), jnp.int32),
        ),
        in_specs=[SMEM, VMEM, VMEM],
        out_specs=(VMEM, VMEM),
        scratch_shapes=[pltpu.VMEM(piece, BF16), pltpu.VMEM(piece, BF16)] + [dma((NB,))] * 6,
        compiler_params=pltpu.CompilerParams(collective_id=0, has_side_effects=True),
    )(owners, valence.reshape(piece), gvec_index.reshape(1, NGD))

    me = lax.axis_index("ga").reshape(1).astype(jnp.int32)
    partial_coeffs = pl.pallas_call(
        compute_kernel,
        out_shape=jax.ShapeDtypeStruct((2, 4, 4, 2 * NF, NGD), F32),
        in_specs=[SMEM] + [VMEM] * 6,
        out_specs=VMEM,
        scratch_shapes=[pltpu.VMEM((64 * KB, 128), F32)],
    )(me, conduction, fields.reshape(NV, 4, NGRID, NGRID), gvecs, ztab, ytab, xtab)

    weights = (1.0 / (val_energy[None, :] - cond_energy[:, None])).reshape(NF, 1)
    weights = jnp.broadcast_to(jnp.concatenate([weights, weights], axis=0), (2 * NF, PANEL))
    spread, panel = pl.pallas_call(
        exchange_kernel,
        out_shape=(
            jax.ShapeDtypeStruct((8, 4, 64, 128), BF16),
            jax.ShapeDtypeStruct((NB, 32, PANEL), BF16),
        ),
        in_specs=[VMEM, VMEM],
        out_specs=(VMEM, VMEM),
        scratch_shapes=[
            pltpu.VMEM((4, 4, 2 * NF, NGD), F32),
            pltpu.VMEM((4, 4, 2 * NF, NGD), F32),
            pltpu.VMEM((4, 4, 2 * NF, NGD), F32),
            pltpu.VMEM((4, 2 * NF, NGD), F32),
            pltpu.VMEM((4, 2 * NF, NGD), F32),
            pltpu.VMEM((64, 128), F32),
            pltpu.VMEM((64, 128), BF16),
            pltpu.VMEM((32, PANEL), BF16),
        ]
        + [dma((4,))] * 8
        + [dma((NB,))] * 2
        + [dma((4, 4))] * 2
        + [dma((8, 4))] * 2,
        compiler_params=pltpu.CompilerParams(collective_id=1, has_side_effects=True),
    )(partial_coeffs, weights)

    return pl.pallas_call(
        chi_kernel,
        out_shape=jax.ShapeDtypeStruct((NGD, PANEL), F32),
        in_specs=[VMEM, VMEM],
        out_specs=VMEM,
        scratch_shapes=[pltpu.VMEM((NB * 24, NGD), F32), pltpu.VMEM((NB * 24, PANEL), F32)],
    )(spread, panel)


def solution(mesh):
    ztab, ytab, xtab = (jnp.asarray(t) for t in tables())

    def step(valence, conduction, owners, val_energy, cond_energy, gvec_index):
        return jax.shard_map(
            per_device,
            mesh=mesh,
            in_specs=(
                P("band", None, "ga", None, None),
                P("band", "ga", None, None),
                P(),
                P(),
                P("band"),
                P("ga"),
                P(),
                P(),
                P(),
            ),
            out_specs=P("band", "ga"),
            check_vma=False,
        )(valence, conduction, owners, val_energy, cond_energy, gvec_index, ztab, ytab, xtab)

    return step
```

time: 696 us -> 125 us (0.18)
  the two profiles are of different devices: /device:TPU:2 before, /device:TPU:1 now
where the time goes in v1:
time: 125 us
  Pallas kernels  122 us (98%)
  local copies, waits for them, and re-layouts  2 us (2%)
    pallas_call x1, Pallas kernels, per_device(): pl.pallas_call(exchange_kernel, out_shape=(jax.ShapeDtypeStruct((8, 4, 64...  52.4 us
    pallas_call x1, Pallas kernels, per_device(): pl.pallas_call(spread_kernel, out_shape=(jax.ShapeDtypeStruct(piece, BF16...  45.9 us
    pallas_call x1, Pallas kernels, per_device(): pl.pallas_call(compute_kernel, out_shape=jax.ShapeDtypeStruct((2, 4, 4, 2...  19.6 us
    pallas_call x1, Pallas kernels, per_device(): pl.pallas_call(chi_kernel, out_shape=jax.ShapeDtypeStruct((NGD, PANEL), F...  4.38 us

profile of v1, /device:TPU:1, one launch (start us, length us, event | category | flops | bytes accessed | tf_op | source)
XLA Modules:
  0.0 125.1 jit_solution(15749402101333044339)
XLA Ops:
  0.0 1.2 reshape.44.gv_ref
  1.2 0.7 subtract_divide_fusion
  2.0 0.1 div.14
  2.1 0.1 maximum_bitcast_fusion
  2.1 0.7 broadcast_in_dim.10.w_ref
  2.8 45.9 %shard_map.91 = (bf16[32,32,128]{2,1,0:T(8,128)(2,1)}, s32[32,1,320]{2,1,0:T(1,128)}) custom-call(s32[2]{0:T(128)} %own_ref.1, bf16[32,32,128]{2,1,0:T(8,128)(2,1)} %bitcast.6, s32[1,320]{1,0:T(1,128)} %reshape.44.gv_ref), custom_call_target="tpu_custom_call" | custom-call | tf_op jit(solution)/shard_map/pallas_call | solution.py:359
  48.8 19.6 %shard_map.92.p_ref = f32[2,4,4,24,320]{4,3,2,1,0:T(8,128)} custom-call(s32[1]{0:T(128)} %bitcast.me_ref, bf16[6,4,128,128]{3,2,1,0:T(8,128)(2,1)} %cond_ref.1, bf16[2,4,128,128]{3,2,1,0:T(8,128)(2,1)} %bitcast.5, s32[32,1,320]{2,1,0:T(1,128)} %get-tuple-element.10.gva_ref, bf16[2,256,256]{2,1,0:T(8,128)(2,1)} %constant.12.clone.zt_ref, ...), custom_call_target="tpu_custom_call" | custom-call | tf_op jit(solution)/shard_map/pallas_call | solution.py:372
  68.4 52.4 %shard_map.93 = (bf16[8,4,64,128]{3,2,1,0:T(8,128)(2,1)}, bf16[32,32,128]{2,1,0:T(8,128)(2,1)}) custom-call(f32[2,4,4,24,320]{4,3,2,1,0:T(8,128)} %shard_map.92.p_ref, f32[24,128]{1,0:T(8,128)} %broadcast_in_dim.10.w_ref), custom_call_target="tpu_custom_call" | custom-call | tf_op jit(solution)/shard_map/pallas_call | solution.py:382
  120.7 4.4 %shard_map.94 = f32[320,128]{1,0:T(8,128)} custom-call(bf16[8,4,64,128]{3,2,1,0:T(8,128)(2,1)} %get-tuple-element.11.r_ref, bf16[32,32,128]{2,1,0:T(8,128)(2,1)} %get-tuple-element.12.wo_ref), custom_call_target="tpu_custom_call" | custom-call | tf_op jit(solution)/shard_map/pallas_call | solution.py:407

commit v2 on v1

v2 whole, which is shorter than its diff:
```python
import math

import jax
import jax.numpy as jnp
import numpy as np
from jax import lax
from jax.experimental import pallas as pl
from jax.experimental.pallas import tpu as pltpu
from jax.sharding import PartitionSpec as P

NGRID = 128
KB = 64
NV = 2
NC = 6
NF = NV * NC
NGD = 320
PANEL = 128
NB = 32
NGA = 32

F32 = jnp.float32
BF16 = jnp.bfloat16
MESH = pl.DeviceIdType.MESH
VMEM = pl.BlockSpec(memory_space=pltpu.VMEM)
SMEM = pl.BlockSpec(memory_space=pltpu.SMEM)


def split_table(table, terms):
    parts = []
    rest = table.astype(np.float32)
    for _ in range(terms):
        part = rest.astype(jnp.bfloat16)
        parts.append(part)
        rest = rest - part.astype(np.float32)
    return parts


def tables():
    n = np.arange(NGRID)[:, None]
    m = np.arange(KB)[None, :] - KB // 2
    angle = ((n * m) % NGRID).astype(np.float64) * (2.0 * math.pi / NGRID)
    scale = 1.0 / math.sqrt(NGRID)
    c = np.cos(angle) * scale
    s = -np.sin(angle) * scale
    zh, zl = split_table(np.concatenate([c, s], axis=1), 2)
    ztab = np.concatenate([np.concatenate([zh, zh], axis=0), np.concatenate([zl, zl], axis=0)], axis=1)
    yh, yl = split_table(np.concatenate([c.T, s.T], axis=0), 2)
    ytab = np.concatenate([np.concatenate([yh, yh], axis=1), np.concatenate([yl, yl], axis=1)], axis=0)
    own = np.concatenate([c.reshape(NGA, 4, KB), s.reshape(NGA, 4, KB)], axis=1)
    parts = split_table(own, 3)
    xtab = np.concatenate(parts + [np.zeros_like(parts[0])], axis=1)
    return ztab, ytab, xtab


def spread_kernel(own_ref, val_ref, gv_ref, out_ref, gva_ref, masked, recv, ss, sr, gs, gr, vs, vr):
    b = lax.axis_index("band")
    a = lax.axis_index("ga")
    barrier = pltpu.get_barrier_semaphore()

    def greet(d, carry):
        pl.semaphore_signal(barrier, 1, device_id=(lax.rem(b + d, NB), a), device_id_type=MESH)
        pl.semaphore_signal(barrier, 1, device_id=(b, lax.rem(a + d, NGA)), device_id_type=MESH)
        return carry

    lax.fori_loop(1, NB, greet, 0)
    half = NB // NV
    for k in range(NV):
        flag = jnp.where(own_ref[k] == b, 1.0, 0.0).astype(F32)
        block = val_ref[k * half : (k + 1) * half].astype(F32)
        masked[k * half : (k + 1) * half] = (block * flag).astype(BF16)
    gva_ref[a] = gv_ref[...].reshape(1, NGD)
    pl.semaphore_wait(barrier, 2 * (NB - 1))

    def piece(p):
        return pltpu.make_async_remote_copy(
            masked.at[p], recv.at[b], ss.at[p], sr.at[b], device_id=(p, a), device_id_type=MESH
        )

    def piece_in(p):
        return pltpu.make_async_remote_copy(
            masked.at[p], recv.at[p], ss.at[p], sr.at[p], device_id=(p, a), device_id_type=MESH
        )

    def whole(p):
        return pltpu.make_async_remote_copy(
            out_ref.at[b], out_ref.at[b], gs.at[p], gr.at[b], device_id=(p, a), device_id_type=MESH
        )

    def whole_in(p):
        return pltpu.make_async_remote_copy(
            out_ref.at[b], out_ref.at[p], gs.at[p], gr.at[p], device_id=(p, a), device_id_type=MESH
        )

    def gvec(q):
        return pltpu.make_async_remote_copy(
            gva_ref.at[a], gva_ref.at[a], vs.at[q], vr.at[a], device_id=(b, q), device_id_type=MESH
        )

    def gvec_in(q):
        return pltpu.make_async_remote_copy(
            gva_ref.at[a], gva_ref.at[q], vs.at[q], vr.at[q], device_id=(b, q), device_id_type=MESH
        )

    def over_band(fn):
        lax.fori_loop(1, NB, lambda d, carry: (fn(lax.rem(b + d, NB)), carry)[1], 0)

    def over_ga(fn):
        lax.fori_loop(1, NGA, lambda d, carry: (fn(lax.rem(a + d, NGA)), carry)[1], 0)

    over_band(lambda p: piece(p).start())
    over_ga(lambda q: gvec(q).start())

    def add(d, total):
        p = lax.rem(b + NB - d, NB)
        piece_in(p).wait_recv()
        return total + recv[p].astype(F32)

    total = lax.fori_loop(1, NB, add, masked[b].astype(F32))
    out_ref[b] = total.astype(BF16)
    over_band(lambda p: whole(p).start())
    over_ga(lambda q: gvec_in(q).wait_recv())
    over_band(lambda p: whole_in(p).wait_recv())
    over_band(lambda p: piece(p).wait_send())
    over_band(lambda p: whole(p).wait_send())
    over_ga(lambda q: gvec(q).wait_send())


def dot(x, y):
    return jnp.dot(x, y, preferred_element_type=F32)


def split(x):
    high = x.astype(BF16)
    return high, (x - high.astype(F32)).astype(BF16)


def dot(x, y):
    return jnp.dot(x, y, preferred_element_type=F32)


def split(x):
    high = x.astype(BF16)
    return high, (x - high.astype(F32)).astype(BF16)


def main_kernel(
    ve_ref, ce_ref, cond_ref, val_ref, gva_ref, zt_ref, yt_ref, xt_ref, out_ref,
    z_scr, y_scr, p_buf, c_rcv, s1, x_rcv, s2, z_rcv, t_buf, w_buf, r_ref, wo_ref, left, right,
    cs, cr, xs, xr, zs, zr, ts, tr, ps, pr, xas, xar, cas, car,
):
    b = lax.axis_index("band")
    a = lax.axis_index("ga")
    zl, y = lax.div(b, 8), lax.rem(b, 8)
    zh, x, c = lax.div(a, 8), lax.rem(lax.div(a, 2), 4), lax.rem(a, 2)
    e = lax.rem(a, 8)
    other = a + 1 - 2 * c
    barrier = pltpu.get_barrier_semaphore()

    def copy(src, dst, send, recv, where):
        return pltpu.make_async_remote_copy(
            src, dst, send, recv, device_id=where, device_id_type=MESH
        )

    def at_x(xx):
        return (b, zh * 8 + xx * 2 + c)

    def at_z(zz):
        return (b, zz * 8 + x * 2 + c)

    def greet(band, ga):
        pl.semaphore_signal(barrier, 1, device_id=(band, ga), device_id_type=MESH)

    for s in range(4):
        source = s * 8 + e

        @pl.when(jnp.logical_or(source != b, a != b))
        def _():
            greet(source, b)

    for d in (2, 1, 3):
        greet(*at_z(lax.rem(zh + d, 4)))
        greet(*at_x(lax.rem(x + d, 4)))
    greet(b, other)

    def greet_band(d, carry):
        greet(lax.rem(b + d, NB), a)
        return carry

    lax.fori_loop(1, NB, greet_band, 0)

    for xl in range(4):
        y_scr[(xl * 16 + NF) * KB : (xl + 1) * 16 * KB, :] = jnp.zeros((4 * KB, 128), F32)
    low = lax.broadcasted_iota(jnp.int32, (1, 128), 1) < KB
    sign = jnp.where(low, -1.0, 1.0).astype(F32)

    def along_z(f):
        pair = cond_ref[lax.div(f, NV)].astype(F32) * val_ref[lax.rem(f, NV)].astype(F32)
        hl = jnp.concatenate(split(pair.reshape(4 * NGRID, NGRID)), axis=1)
        both = dot(hl, zt_ref[...])
        high, rest = split(both[:, :128] + both[:, 128:])
        for xl in range(4):
            rows = slice(xl * NGRID, (xl + 1) * NGRID)
            z_scr[xl // 2, 0:NGRID, (xl % 2) * 128 : (xl % 2 + 1) * 128] = high[rows]
            z_scr[xl // 2, NGRID : 2 * NGRID, (xl % 2) * 128 : (xl % 2 + 1) * 128] = rest[rows]

    def along_y(f):
        for pair in range(2):
            both = dot(yt_ref[...], z_scr[pair])
            sums = both[:128] + both[128:]
            for i in range(2):
                part = sums[:, i * 128 : (i + 1) * 128]
                row = pl.multiple_of(((2 * pair + i) * 16 + f) * KB, KB)
                y_scr[pl.ds(row, KB), :] = part[:KB] + pltpu.roll(part[KB:], KB, 1) * sign

    def field(f, carry):
        along_y(f - 1)
        along_z(f)
        return carry

    along_z(0)
    lax.fori_loop(1, NF, field, 0)
    along_y(NF - 1)

    xt = xt_ref[a]
    lane = lax.broadcasted_iota(jnp.int32, (64, 128), 1) < KB
    cell = lax.broadcasted_iota(jnp.int32, (128, NGD), 0)
    xcell = lax.broadcasted_iota(jnp.int32, (KB, NGD), 0)

    def select(zz, xx, cc):
        j = zz * 8 + xx * 2 + cc
        y0 = y_scr[pl.ds(2 * j, 64, stride=KB), :]
        y1 = y_scr[pl.ds(2 * j + 1, 64, stride=KB), :]
        ur = jnp.where(lane, y0, pltpu.roll(y1, KB, 1))
        ui = jnp.where(lane, pltpu.roll(y0, KB, 1), y1)
        hl = jnp.concatenate(split(jnp.concatenate([ur, ui], axis=0)), axis=1)
        v = gva_ref[j]
        hot = jnp.where(cell == (v & 127), 1.0, 0.0).astype(BF16)
        xhot = jnp.where(xcell == (v >> 7), 1.0, 0.0).astype(BF16)
        sel = dot(hl, jnp.concatenate([hot, hot], axis=0))
        e3 = dot(xt, xhot)
        phase = e3[0:8] + (e3[8:16] + e3[16:24])
        re = jnp.zeros((16, NGD), F32)
        im = jnp.zeros((16, NGD), F32)
        for xl in range(4):
            sr = sel[xl * 16 : (xl + 1) * 16]
            si = sel[64 + xl * 16 : 64 + (xl + 1) * 16]
            er = phase[xl : xl + 1]
            ei = phase[4 + xl : 5 + xl]
            re = re + (sr * er - si * ei)
            im = im + (si * er + sr * ei)
        rows = jnp.concatenate([re[:NF], im[:NF]], axis=0)
        p_buf[cc, zz, xx, 0:24] = rows[:, 0:128]
        p_buf[cc, zz, xx, 24:48] = rows[:, 128:256]
        p_buf[cc, zz, xx, 48:64, 0:64] = rows[0:16, 256:320]
        p_buf[cc, zz, xx, 48:56, 64:128] = rows[16:24, 256:320]
        p_buf[cc, zz, xx, 56:64, 64:128] = jnp.zeros((8, 64), F32)

    def select_group(zz):
        def pair(xx, carry):
            select(zz, xx, 1 - c)
            select(zz, xx, c)
            return carry

        lax.fori_loop(0, 4, pair, 0)

    x_order = [lax.rem(x + d, 4) for d in (2, 1, 3)]
    z_order = [lax.rem(zh + d, 4) for d in (2, 1, 3)] + [zh]

    def to_core(zz):
        return copy(p_buf.at[1 - c, zz], c_rcv.at[zz], cs.at[zz], cr.at[zz], (b, other))

    def to_x(zz, xx):
        return copy(s1.at[zz, xx], x_rcv.at[x, zz], xs.at[xx, zz], xr.at[x, zz], at_x(xx))

    def from_x(zz, xx):
        return copy(s1.at[zz, xx], x_rcv.at[xx, zz], xs.at[xx, zz], xr.at[xx, zz], at_x(xx))

    def to_z(zz):
        return copy(s2.at[zz], z_rcv.at[zh], zs.at[zz], zr.at[zh], at_z(zz))

    def from_z(zz):
        return copy(s2.at[zz], z_rcv.at[zz], zs.at[zz], zr.at[zz], at_z(zz))

    def core_done(zz):
        to_core(zz).wait_recv()
        s1[zz] = p_buf[c, zz] + c_rcv[zz]
        for xx in x_order:
            to_x(zz, xx).start()

    def x_done(zz):
        for xx in x_order:
            from_x(zz, xx).wait_recv()
        s2[zz] = (s1[zz, x] + x_rcv[x_order[0], zz]) + (x_rcv[x_order[1], zz] + x_rcv[x_order[2], zz])

    for i, zz in enumerate(z_order):
        select_group(zz)
        if i == 0:
            pl.semaphore_wait(barrier, 38 + 4 - jnp.where(a == b, 1, 0))
        to_core(zz).start()
        if i:
            core_done(z_order[i - 1])
    core_done(zh)
    for zz in z_order[:3]:
        x_done(zz)
        to_z(zz).start()
    x_done(zh)
    row = lax.rem(lax.broadcasted_iota(jnp.int32, (24, PANEL), 0), NF)
    ve = jnp.where(lax.rem(row, NV) == 0, ve_ref[0], ve_ref[1])
    ce = jnp.full((24, PANEL), ce_ref[0], F32)
    for i in range(1, NC):
        ce = jnp.where(lax.div(row, NV) == i, ce_ref[i], ce)
    weights = 1.0 / (ve - ce)
    for zz in z_order[:3]:
        from_z(zz).wait_recv()
    total = (s2[zh] + z_rcv[z_order[0]]) + (z_rcv[z_order[1]] + z_rcv[z_order[2]])
    coeffs = total.astype(BF16)
    t_buf[...] = coeffs
    for zz in z_order:
        target = zz * 8 + y
        stays = jnp.logical_and(a == b, target == a)

        @pl.when(jnp.logical_not(stays))
        def _():
            copy(t_buf, r_ref.at[y, zl], ts.at[zz], tr.at[zl], (a, target)).start()

        @pl.when(stays)
        def _():
            pltpu.make_async_copy(t_buf, r_ref.at[y, zl], tr.at[zl]).start()

    weighted = coeffs.astype(F32)[0:24] * weights
    weighted = jnp.concatenate([weighted, jnp.zeros((8, PANEL), F32)], axis=0).astype(BF16)
    w_buf[...] = weighted
    wo_ref[b] = weighted

    def panel(p):
        return copy(w_buf, wo_ref.at[b], ps.at[p], pr.at[b], (p, a))

    def panel_in(p):
        return copy(w_buf, wo_ref.at[p], ps.at[p], pr.at[p], (p, a))

    def over_band(fn):
        lax.fori_loop(1, NB, lambda d, carry: (fn(lax.rem(b + d, NB)), carry)[1], 0)

    over_band(lambda p: panel(p).start())

    def along_x(ee, src_x, xx, s):
        return copy(r_ref.at[ee, s], r_ref.at[ee, s], xas.at[xx, s], xar.at[src_x, s], at_x(xx))

    def along_core(ee, s):
        return copy(r_ref.at[ee, s], r_ref.at[ee, s], cas.at[ee, s], car.at[ee, s], (b, other))

    def place(base, ee, s):
        at = (base + s) * 24
        block = r_ref[ee, s].astype(F32)
        left[at : at + 24, 0:128] = block[0:24]
        left[at : at + 24, 128:256] = block[24:48]
        left[at : at + 16, 256:320] = block[48:64, 0:64]
        left[at + 16 : at + 24, 256:320] = block[48:56, 64:128]

    def place_weighted(base, ee):
        for s in range(4):
            at = (base + s) * 24
            right[at : at + 24, :] = wo_ref[s * 8 + ee].astype(F32)[0:24]

    def product(half):
        rows = slice(half * 384, (half + 1) * 384)
        return lax.dot_general(
            left[rows].astype(BF16),
            right[rows].astype(BF16),
            (((0,), (0,)), ((), ())),
            preferred_element_type=F32,
        )

    for s in range(4):
        pltpu.make_async_copy(t_buf, r_ref.at[e, s], tr.at[s]).wait()
        for xx in x_order:
            along_x(e, x, xx, s).start()
        along_core(e, s).start()
        place(0, e, s)
    for s in range(4):
        for i, xx in enumerate(x_order):
            ee = xx * 2 + c
            along_x(ee, xx, xx, s).wait_recv()
            along_core(ee, s).start()
            place(4 + 4 * i, ee, s)
    over_band(lambda p: panel_in(p).wait_recv())
    for i, xx in enumerate([x] + x_order):
        place_weighted(4 * i, xx * 2 + c)
        place_weighted(16 + 4 * i, xx * 2 + 1 - c)
    chi = product(0)
    for i, xx in enumerate([x] + x_order):
        for s in range(4):
            along_core(xx * 2 + 1 - c, s).wait_recv()
            place(16 + 4 * i, xx * 2 + 1 - c, s)
    out_ref[...] = chi + product(1)
    for zz in z_order:
        to_core(zz).wait_send()
        for xx in x_order:
            to_x(zz, xx).wait_send()
    for zz in z_order[:3]:
        to_z(zz).wait_send()
    for zz in z_order:
        target = zz * 8 + y

        @pl.when(jnp.logical_not(jnp.logical_and(a == b, target == a)))
        def _():
            copy(t_buf, r_ref.at[y, zl], ts.at[zz], tr.at[zl], (a, target)).wait_send()

    over_band(lambda p: panel(p).wait_send())
    for s in range(4):
        for xx in x_order:
            along_x(e, x, xx, s).wait_send()
        for xx in [x] + x_order:
            along_core(xx * 2 + c, s).wait_send()


def per_device(valence, conduction, owners, val_energy, cond_energy, gvec_index, ztab, ytab, xtab):
    dma = pltpu.SemaphoreType.DMA
    piece = (NB, 32, 128)
    fields, gvecs = pl.pallas_call(
        spread_kernel,
        out_shape=(
            jax.ShapeDtypeStruct(piece, BF16),
            jax.ShapeDtypeStruct((NGA, 1, NGD), jnp.int32),
        ),
        in_specs=[SMEM, VMEM, VMEM],
        out_specs=(VMEM, VMEM),
        scratch_shapes=[pltpu.VMEM(piece, BF16), pltpu.VMEM(piece, BF16)] + [dma((NB,))] * 6,
        compiler_params=pltpu.CompilerParams(collective_id=0, has_side_effects=True),
    )(owners, valence.reshape(piece), gvec_index)

    tile = (64, 128)
    return pl.pallas_call(
        main_kernel,
        out_shape=jax.ShapeDtypeStruct((NGD, PANEL), F32),
        in_specs=[SMEM, SMEM] + [VMEM] * 6,
        out_specs=VMEM,
        scratch_shapes=[
            pltpu.VMEM((2, 2 * NGRID, 2 * NGRID), BF16),
            pltpu.VMEM((64 * KB, 128), F32),
            pltpu.VMEM((2, 4, 4) + tile, F32),
            pltpu.VMEM((4, 4) + tile, F32),
            pltpu.VMEM((4, 4) + tile, F32),
            pltpu.VMEM((4, 4) + tile, F32),
            pltpu.VMEM((4,) + tile, F32),
            pltpu.VMEM((4,) + tile, F32),
            pltpu.VMEM(tile, BF16),
            pltpu.VMEM((32, PANEL), BF16),
            pltpu.VMEM((8, 4) + tile, BF16),
            pltpu.VMEM((NB, 32, PANEL), BF16),
            pltpu.VMEM((NB * 24, NGD), F32),
            pltpu.VMEM((NB * 24, PANEL), F32),
            dma((4,)),
            dma((4,)),
            dma((4, 4)),
            dma((4, 4)),
            dma((4,)),
            dma((4,)),
            dma((4,)),
            dma((4,)),
            dma((NB,)),
            dma((NB,)),
            dma((4, 4)),
            dma((4, 4)),
            dma((8, 4)),
            dma((8, 4)),
        ],
        compiler_params=pltpu.CompilerParams(collective_id=1, has_side_effects=True),
    )(
        val_energy, cond_energy, conduction, fields.reshape(NV, 4, NGRID, NGRID), gvecs, ztab, ytab, xtab
    )


def solution(mesh):
    ztab, ytab, xtab = (jnp.asarray(t) for t in tables())

    def step(valence, conduction, owners, val_energy, cond_energy, gvec_index):
        return jax.shard_map(
            per_device,
            mesh=mesh,
            in_specs=(
                P("band", None, "ga", None, None),
                P("band", "ga", None, None),
                P(),
                P(),
                P("band"),
                P("ga"),
                P(),
                P(),
                P(),
            ),
            out_specs=P("band", "ga"),
            check_vma=False,
        )(valence, conduction, owners, val_energy, cond_energy, gvec_index, ztab, ytab, xtab)

    return step
```

time: 125 us -> 99.9 us (0.80)
  Pallas kernels: 122 us -> 98 us
    pallas_call x3 -> x1, Pallas kernels: 76.3 us -> 52.1 us  [per_device(): pl.pallas_call(main_kernel, out_shape=jax.ShapeDtypeStruct((NGD, PANEL),...]
    unnamed x0 -> x1, local copies, waits for them, and re-layouts: none -> 1.59 us
where the time goes in v2:
time: 99.9 us; the launch traced here: 99.6 us
  Pallas kernels  98 us (98%)
  local copies, waits for them, and re-layouts  1.59 us (2%)
    pallas_call x1, Pallas kernels, per_device(): pl.pallas_call(main_kernel, out_shape=jax.ShapeDtypeStruct((NGD, PANEL),...  52.1 us
    pallas_call x1, Pallas kernels, per_device(): pl.pallas_call(spread_kernel, out_shape=(jax.ShapeDtypeStruct(piece, BF16...  45.9 us

profile of v2, /device:TPU:1, one launch (start us, length us, event | category | flops | bytes accessed | tf_op | source)
XLA Modules:
  0.0 99.6 jit_solution(12800053350591610228)
XLA Ops:
  0.0 45.9 %shard_map.91 = (bf16[32,32,128]{2,1,0:T(8,128)(2,1)}, s32[32,1,320]{2,1,0:T(1,128)}) custom-call(s32[2]{0:T(128)} %own_ref.1, bf16[32,32,128]{2,1,0:T(8,128)(2,1)} %bitcast.3, s32[320]{0:T(512)} %gv_ref.1), custom_call_target="tpu_custom_call" | custom-call | tf_op jit(solution)/shard_map/pallas_call | solution.py:420
  45.9 52.1 %shard_map.92 = f32[320,128]{1,0:T(8,128)} custom-call(f32[2]{0:T(128)} %ve_ref.1, f32[6]{0:T(128)} %ce_ref.1, bf16[6,4,128,128]{3,2,1,0:T(8,128)(2,1)} %cond_ref.1, bf16[2,4,128,128]{3,2,1,0:T(8,128)(2,1)} %bitcast.2, s32[32,1,320]{2,1,0:T(1,128)} %get-tuple-element.8.gva_ref, bf16[256,256]{1,0:T(8,128)(2,1)} %constant.6.clone.zt_ref, ...), custom_call_target="tpu_custom_call" | custom-call | tf_op jit(solution)/shard_map/pallas_call | solution.py:433
  98.0 1.6 %copy.11 = f32[320,128]{1,0:T(8,128)} copy(f32[320,128]{1,0:T(8,128)} %shard_map.92) | data formatting | bytes 327680

commit v3 on v2

--- a/solution.py
+++ b/solution.py
@@ -52,79 +52,6 @@
     return ztab, ytab, xtab
 
 
-def spread_kernel(own_ref, val_ref, gv_ref, out_ref, gva_ref, masked, recv, ss, sr, gs, gr, vs, vr):
-    b = lax.axis_index("band")
-    a = lax.axis_index("ga")
-    barrier = pltpu.get_barrier_semaphore()
-
-    def greet(d, carry):
-        pl.semaphore_signal(barrier, 1, device_id=(lax.rem(b + d, NB), a), device_id_type=MESH)
-        pl.semaphore_signal(barrier, 1, device_id=(b, lax.rem(a + d, NGA)), device_id_type=MESH)
-        return carry
-
-    lax.fori_loop(1, NB, greet, 0)
-    half = NB // NV
-    for k in range(NV):
-        flag = jnp.where(own_ref[k] == b, 1.0, 0.0).astype(F32)
-        block = val_ref[k * half : (k + 1) * half].astype(F32)
-        masked[k * half : (k + 1) * half] = (block * flag).astype(BF16)
-    gva_ref[a] = gv_ref[...].reshape(1, NGD)
-    pl.semaphore_wait(barrier, 2 * (NB - 1))
-
-    def piece(p):
-        return pltpu.make_async_remote_copy(
-            masked.at[p], recv.at[b], ss.at[p], sr.at[b], device_id=(p, a), device_id_type=MESH
-        )
-
-    def piece_in(p):
-        return pltpu.make_async_remote_copy(
-            masked.at[p], recv.at[p], ss.at[p], sr.at[p], device_id=(p, a), device_id_type=MESH
-        )
-
-    def whole(p):
-        return pltpu.make_async_remote_copy(
-            out_ref.at[b], out_ref.at[b], gs.at[p], gr.at[b], device_id=(p, a), device_id_type=MESH
-        )
-
-    def whole_in(p):
-        return pltpu.make_async_remote_copy(
-            out_ref.at[b], out_ref.at[p], gs.at[p], gr.at[p], device_id=(p, a), device_id_type=MESH
-        )
-
-    def gvec(q):
-        return pltpu.make_async_remote_copy(
-            gva_ref.at[a], gva_ref.at[a], vs.at[q], vr.at[a], device_id=(b, q), device_id_type=MESH
-        )
-
-    def gvec_in(q):
-        return pltpu.make_async_remote_copy(
-            gva_ref.at[a], gva_ref.at[q], vs.at[q], vr.at[q], device_id=(b, q), device_id_type=MESH
-        )
-
-    def over_band(fn):
-        lax.fori_loop(1, NB, lambda d, carry: (fn(lax.rem(b + d, NB)), carry)[1], 0)
-
-    def over_ga(fn):
-        lax.fori_loop(1, NGA, lambda d, carry: (fn(lax.rem(a + d, NGA)), carry)[1], 0)
-
-    over_band(lambda p: piece(p).start())
-    over_ga(lambda q: gvec(q).start())
-
-    def add(d, total):
-        p = lax.rem(b + NB - d, NB)
-        piece_in(p).wait_recv()
-        return total + recv[p].astype(F32)
-
-    total = lax.fori_loop(1, NB, add, masked[b].astype(F32))
-    out_ref[b] = total.astype(BF16)
-    over_band(lambda p: whole(p).start())
-    over_ga(lambda q: gvec_in(q).wait_recv())
-    over_band(lambda p: whole_in(p).wait_recv())
-    over_band(lambda p: piece(p).wait_send())
-    over_band(lambda p: whole(p).wait_send())
-    over_ga(lambda q: gvec(q).wait_send())
-
-
 def dot(x, y):
     return jnp.dot(x, y, preferred_element_type=F32)
 
@@ -144,8 +71,10 @@
 
 
 def main_kernel(
-    ve_ref, ce_ref, cond_ref, val_ref, gva_ref, zt_ref, yt_ref, xt_ref, out_ref,
+    own_ref, ve_ref, ce_ref, val_ref, gv_ref, cond_hbm, zt_ref, yt_ref, xt_ref, out_ref,
+    cond_ref, masked, pieces, fields, gva, hots, phases,
     z_scr, y_scr, p_buf, c_rcv, s1, x_rcv, s2, z_rcv, t_buf, w_buf, r_ref, wo_ref, left, right,
+    load, ss, sr, gs, gr, vzs, vzr, vxs, vxr, vcs, vcr,
     cs, cr, xs, xr, zs, zr, ts, tr, ps, pr, xas, xar, cas, car,
 ):
     b = lax.axis_index("band")
@@ -182,20 +111,106 @@
         greet(*at_x(lax.rem(x + d, 4)))
     greet(b, other)
 
-    def greet_band(d, carry):
-        greet(lax.rem(b + d, NB), a)
-        return carry
-
-    lax.fori_loop(1, NB, greet_band, 0)
-
+    def over_band(fn):
+        def step(i, carry):
+            u = lax.div(i, 4)
+            dy = 4 + (1 - 2 * lax.rem(u, 2)) * lax.div(u + 1, 2)
+            fn(lax.rem(zl + 1 + lax.rem(i, 4), 4) * 8 + lax.rem(y + dy, 8))
+            return carry
+
+        lax.fori_loop(0, NB - 1, step, 0)
+
+    over_band(lambda p: greet(p, a))
+    fetch = pltpu.make_async_copy(cond_hbm, cond_ref, load)
+    fetch.start()
+
+    for k in range(NV):
+        flag = jnp.where(own_ref[k] == b, 1.0, 0.0).astype(F32)
+        masked[k] = (val_ref[k].astype(F32) * flag).astype(BF16)
+        pieces[k, b] = masked[k, b]
+    mine = c * 16 + x * 4 + zh
+    gva[mine] = gv_ref[...].reshape(1, NGD)
     for xl in range(4):
         y_scr[(xl * 16 + NF) * KB : (xl + 1) * 16 * KB, :] = jnp.zeros((4 * KB, 128), F32)
+
+    x_order = [lax.rem(x + d, 4) for d in (2, 1, 3)]
+    z_order = [lax.rem(zh + d, 4) for d in (2, 1, 3)] + [zh]
+
+    def piece(k, p):
+        return copy(masked.at[k, p], pieces.at[k, b], ss.at[k], sr.at[k], (p, a))
+
+    def whole(k, p):
+        return copy(fields.at[k, b], fields.at[k, b], gs.at[k], gr.at[k], (p, a))
+
+    def all_pieces(k):
+        return copy(masked.at[k, pl.ds(0, NB - 1)], pieces.at[k, pl.ds(0, NB - 1)], ss.at[k], sr.at[k], (b, other))
+
+    def all_whole(k):
+        return copy(fields.at[k, pl.ds(0, NB - 1)], fields.at[k, pl.ds(0, NB - 1)], gs.at[k], gr.at[k], (b, other))
+
+    def g_z(zz, slot):
+        return copy(gva.at[mine], gva.at[c * 16 + x * 4 + slot], vzs.at[zz], vzr.at[slot], at_z(zz))
+
+    def g_x(xx, slot):
+        return copy(
+            gva.at[pl.ds(c * 16 + x * 4, 4)], gva.at[pl.ds(c * 16 + slot * 4, 4)], vxs.at[xx], vxr.at[slot], at_x(xx)
+        )
+
+    def g_core(slot):
+        return copy(gva.at[pl.ds(c * 16, 16)], gva.at[pl.ds(slot * 16, 16)], vcs, vcr, (b, other))
+
+    pl.semaphore_wait(barrier, 38 + 4 - jnp.where(a == b, 1, 0))
+    over_band(lambda p: piece(0, p).start())
+    for zz in z_order[:3]:
+        g_z(zz, zh).start()
+    over_band(lambda p: piece(1, p).start())
+    for k in range(NV):
+        all_pieces(k).wait_recv()
+        total = pieces[k, 0].astype(F32)
+        for s in range(1, NB):
+            total = total + pieces[k, s].astype(F32)
+        fields[k, b] = total.astype(BF16)
+        over_band(lambda p: whole(k, p).start())
+        if k == 0:
+            for zz in z_order[:3]:
+                g_z(zz, zz).wait_recv()
+            for xx in x_order:
+                g_x(xx, x).start()
+    for xx in x_order:
+        g_x(xx, xx).wait_recv()
+    g_core(c).start()
+    all_pieces(0).wait_send()
+    all_pieces(1).wait_send()
+
+    xt = xt_ref[a]
+    cell = lax.broadcasted_iota(jnp.int32, (128, NGD), 0)
+    xcell = lax.broadcasted_iota(jnp.int32, (KB, NGD), 0)
+
+    def prepare(j, carry):
+        v = gva[j]
+        hots[j] = jnp.where(cell == (v & 127), 1.0, 0.0).astype(BF16)
+        xhot = jnp.where(xcell == (v >> 7), 1.0, 0.0).astype(BF16)
+        e3 = dot(xt, xhot)
+        phases[j] = e3[0:8] + (e3[8:16] + e3[16:24])
+        return carry
+
+    lax.fori_loop(c * 16, c * 16 + 16, prepare, 0)
+    g_core(1 - c).wait_recv()
+    lax.fori_loop((1 - c) * 16, (1 - c) * 16 + 16, prepare, 0)
+    for zz in z_order[:3]:
+        g_z(zz, zh).wait_send()
+    for xx in x_order:
+        g_x(xx, x).wait_send()
+    g_core(c).wait_send()
+    fetch.wait()
+
     low = lax.broadcasted_iota(jnp.int32, (1, 128), 1) < KB
     sign = jnp.where(low, -1.0, 1.0).astype(F32)
 
-    def along_z(f):
-        pair = cond_ref[lax.div(f, NV)].astype(F32) * val_ref[lax.rem(f, NV)].astype(F32)
-        hl = jnp.concatenate(split(pair.reshape(4 * NGRID, NGRID)), axis=1)
+    def along_z(g):
+        wave = cond_ref[lax.rem(g, NC)].astype(F32).reshape(4 * NGRID, NGRID)
+        pair = wave * fields[lax.div(g, NC)].astype(F32).reshape(4 * NGRID, NGRID)
+        hl = jnp.concatenate(split(pair), axis=1)
         both = dot(hl, zt_ref[...])
         high, rest = split(both[:, :128] + both[:, 128:])
         for xl in range(4):
@@ -203,7 +218,8 @@
             z_scr[xl // 2, 0:NGRID, (xl % 2) * 128 : (xl % 2 + 1) * 128] = high[rows]
             z_scr[xl // 2, NGRID : 2 * NGRID, (xl % 2) * 128 : (xl % 2 + 1) * 128] = rest[rows]
 
-    def along_y(f):
+    def along_y(g):
+        f = lax.rem(g, NC) * NV + lax.div(g, NC)
         for pair in range(2):
             both = dot(yt_ref[...], z_scr[pair])
             sums = both[:128] + both[128:]
@@ -217,14 +233,16 @@
         along_z(f)
         return carry
 
+    all_whole(0).wait_recv()
     along_z(0)
-    lax.fori_loop(1, NF, field, 0)
+    lax.fori_loop(1, NC, field, 0)
+    all_whole(1).wait_recv()
+    lax.fori_loop(NC, NF, field, 0)
     along_y(NF - 1)
-
-    xt = xt_ref[a]
+    all_whole(0).wait_send()
+    all_whole(1).wait_send()
+
     lane = lax.broadcasted_iota(jnp.int32, (64, 128), 1) < KB
-    cell = lax.broadcasted_iota(jnp.int32, (128, NGD), 0)
-    xcell = lax.broadcasted_iota(jnp.int32, (KB, NGD), 0)
 
     def select(zz, xx, cc):
         j = zz * 8 + xx * 2 + cc
@@ -233,12 +251,10 @@
         ur = jnp.where(lane, y0, pltpu.roll(y1, KB, 1))
         ui = jnp.where(lane, pltpu.roll(y0, KB, 1), y1)
         hl = jnp.concatenate(split(jnp.concatenate([ur, ui], axis=0)), axis=1)
-        v = gva_ref[j]
-        hot = jnp.where(cell == (v & 127), 1.0, 0.0).astype(BF16)
-        xhot = jnp.where(xcell == (v >> 7), 1.0, 0.0).astype(BF16)
+        slot = cc * 16 + xx * 4 + zz
+        hot = hots[slot]
         sel = dot(hl, jnp.concatenate([hot, hot], axis=0))
-        e3 = dot(xt, xhot)
-        phase = e3[0:8] + (e3[8:16] + e3[16:24])
+        phase = phases[slot]
         re = jnp.zeros((16, NGD), F32)
         im = jnp.zeros((16, NGD), F32)
         for xl in range(4):
@@ -263,9 +279,6 @@
 
         lax.fori_loop(0, 4, pair, 0)
 
-    x_order = [lax.rem(x + d, 4) for d in (2, 1, 3)]
-    z_order = [lax.rem(zh + d, 4) for d in (2, 1, 3)] + [zh]
-
     def to_core(zz):
         return copy(p_buf.at[1 - c, zz], c_rcv.at[zz], cs.at[zz], cr.at[zz], (b, other))
 
@@ -294,8 +307,6 @@
 
     for i, zz in enumerate(z_order):
         select_group(zz)
-        if i == 0:
-            pl.semaphore_wait(barrier, 38 + 4 - jnp.where(a == b, 1, 0))
         to_core(zz).start()
         if i:
             core_done(z_order[i - 1])
@@ -333,15 +344,18 @@
     wo_ref[b] = weighted
 
     def panel(p):
-        return copy(w_buf, wo_ref.at[b], ps.at[p], pr.at[b], (p, a))
-
-    def panel_in(p):
-        return copy(w_buf, wo_ref.at[p], ps.at[p], pr.at[p], (p, a))
-
-    def over_band(fn):
-        lax.fori_loop(1, NB, lambda d, carry: (fn(lax.rem(b + d, NB)), carry)[1], 0)
+        return copy(w_buf, wo_ref.at[b], ps, pr, (p, a))
+
+    def all_panels():
+        return copy(wo_ref.at[pl.ds(0, NB - 1)], wo_ref.at[pl.ds(0, NB - 1)], ps, pr, (b, other))
 
     over_band(lambda p: panel(p).start())
+    for zz in z_order:
+        to_core(zz).wait_send()
+        for xx in x_order:
+            to_x(zz, xx).wait_send()
+    for zz in z_order[:3]:
+        to_z(zz).wait_send()
 
     def along_x(ee, src_x, xx, s):
         return copy(r_ref.at[ee, s], r_ref.at[ee, s], xas.at[xx, s], xar.at[src_x, s], at_x(xx))
@@ -383,30 +397,24 @@
             along_x(ee, xx, xx, s).wait_recv()
             along_core(ee, s).start()
             place(4 + 4 * i, ee, s)
-    over_band(lambda p: panel_in(p).wait_recv())
+    all_panels().wait_recv()
     for i, xx in enumerate([x] + x_order):
         place_weighted(4 * i, xx * 2 + c)
         place_weighted(16 + 4 * i, xx * 2 + 1 - c)
+    for zz in z_order:
+        target = zz * 8 + y
+
+        @pl.when(jnp.logical_not(jnp.logical_and(a == b, target == a)))
+        def _():
+            copy(t_buf, r_ref.at[y, zl], ts.at[zz], tr.at[zl], (a, target)).wait_send()
+
+    all_panels().wait_send()
     chi = product(0)
     for i, xx in enumerate([x] + x_order):
         for s in range(4):
             along_core(xx * 2 + 1 - c, s).wait_recv()
             place(16 + 4 * i, xx * 2 + 1 - c, s)
     out_ref[...] = chi + product(1)
-    for zz in z_order:
-        to_core(zz).wait_send()
-        for xx in x_order:
-            to_x(zz, xx).wait_send()
-    for zz in z_order[:3]:
-        to_z(zz).wait_send()
-    for zz in z_order:
-        target = zz * 8 + y
-
-        @pl.when(jnp.logical_not(jnp.logical_and(a == b, target == a)))
-        def _():
-            copy(t_buf, r_ref.at[y, zl], ts.at[zz], tr.at[zl], (a, target)).wait_send()
-
-    over_band(lambda p: panel(p).wait_send())
     for s in range(4):
         for xx in x_order:
             along_x(e, x, xx, s).wait_send()
@@ -416,26 +424,21 @@
 
 def per_device(valence, conduction, owners, val_energy, cond_energy, gvec_index, ztab, ytab, xtab):
     dma = pltpu.SemaphoreType.DMA
-    piece = (NB, 32, 128)
-    fields, gvecs = pl.pallas_call(
-        spread_kernel,
-        out_shape=(
-            jax.ShapeDtypeStruct(piece, BF16),
-            jax.ShapeDtypeStruct((NGA, 1, NGD), jnp.int32),
-        ),
-        in_specs=[SMEM, VMEM, VMEM],
-        out_specs=(VMEM, VMEM),
-        scratch_shapes=[pltpu.VMEM(piece, BF16), pltpu.VMEM(piece, BF16)] + [dma((NB,))] * 6,
-        compiler_params=pltpu.CompilerParams(collective_id=0, has_side_effects=True),
-    )(owners, valence.reshape(piece), gvec_index)
-
+    piece = (NV, NB, 16, 128)
     tile = (64, 128)
     return pl.pallas_call(
         main_kernel,
         out_shape=jax.ShapeDtypeStruct((NGD, PANEL), F32),
-        in_specs=[SMEM, SMEM] + [VMEM] * 6,
+        in_specs=[SMEM] * 3 + [VMEM] * 2 + [pl.BlockSpec(memory_space=pl.ANY)] + [VMEM] * 3,
         out_specs=VMEM,
         scratch_shapes=[
+            pltpu.VMEM((NC, 4, NGRID, NGRID), BF16),
+            pltpu.VMEM(piece, BF16),
+            pltpu.VMEM(piece, BF16),
+            pltpu.VMEM(piece, BF16),
+            pltpu.VMEM((NGA, 1, NGD), jnp.int32),
+            pltpu.VMEM((NGA, 128, NGD), BF16),
+            pltpu.VMEM((NGA, 8, NGD), F32),
             pltpu.VMEM((2, 2 * NGRID, 2 * NGRID), BF16),
             pltpu.VMEM((64 * KB, 128), F32),
             pltpu.VMEM((2, 4, 4) + tile, F32),
@@ -450,6 +453,17 @@
             pltpu.VMEM((NB, 32, PANEL), BF16),
             pltpu.VMEM((NB * 24, NGD), F32),
             pltpu.VMEM((NB * 24, PANEL), F32),
+            dma,
+            dma((NV,)),
+            dma((NV,)),
+            dma((NV,)),
+            dma((NV,)),
+            dma((4,)),
+            dma((4,)),
+            dma((4,)),
+            dma((4,)),
+            dma,
+            dma,
             dma((4,)),
             dma((4,)),
             dma((4, 4)),
@@ -458,8 +472,8 @@
             dma((4,)),
             dma((4,)),
             dma((4,)),
-            dma((NB,)),
-            dma((NB,)),
+            dma,
+            dma,
             dma((4, 4)),
             dma((4, 4)),
             dma((8, 4)),
@@ -467,7 +481,7 @@
         ],
         compiler_params=pltpu.CompilerParams(collective_id=1, has_side_effects=True),
     )(
-        val_energy, cond_energy, conduction, fields.reshape(NV, 4, NGRID, NGRID), gvecs, ztab, ytab, xtab
+        owners, val_energy, cond_energy, valence.reshape(piece), gvec_index, conduction, ztab, ytab, xtab
     )
 
 

time: 99.9 us -> 88.7 us (0.89)
  Pallas kernels: 98 us -> 86.9 us
    pallas_call x1 -> x0, Pallas kernels: 45.9 us -> none  [per_device(): pl.pallas_call(spread_kernel, out_shape=(jax.ShapeDtypeStruct(piece, BF16...]
    pallas_call x1, Pallas kernels: 52.1 us -> 86.9 us  [per_device(): pl.pallas_call(main_kernel, out_shape=jax.ShapeDtypeStruct((NGD, PANEL),...]
where the time goes in v3:
time: 88.7 us; the launch traced here: 88.5 us
  Pallas kernels  86.9 us (98%)
  local copies, waits for them, and re-layouts  1.59 us (2%)
    pallas_call x1, Pallas kernels, per_device(): pl.pallas_call(main_kernel, out_shape=jax.ShapeDtypeStruct((NGD, PANEL),...  86.9 us

profile of v3, /device:TPU:1, one launch (start us, length us, event | category | flops | bytes accessed | tf_op | source)
XLA Modules:
  0.0 88.5 jit_solution(13891455641438920263)
XLA Ops:
  0.0 86.9 %shard_map.91 = f32[320,128]{1,0:T(8,128)} custom-call(s32[2]{0:T(128)} %own_ref.1, f32[2]{0:T(128)} %ve_ref.1, f32[6]{0:T(128)} %ce_ref.1, bf16[2,32,16,128]{3,2,1,0:T(8,128)(2,1)} %bitcast.1, s32[320]{0:T(512)} %gv_ref.1, bf16[6,4,128,128]{3,2,1,0:T(8,128)(2,1)} %cond_hbm.1, bf16[256,256]{1,0:T(8,128)(2,1)} %constant.6.clone.zt_ref, ...), custom_call_target="tpu_custom_call" | custom-call | tf_op jit(solution)/shard_map/pallas_call | solution.py:429
  86.9 1.6 %copy.11 = f32[320,128]{1,0:T(8,128)} copy(f32[320,128]{1,0:T(8,128)} %shard_map.91) | data formatting | bytes 327680

commit v4 on v3

--- a/solution.py
+++ b/solution.py
@@ -71,10 +71,10 @@
 
 
 def main_kernel(
-    own_ref, ve_ref, ce_ref, val_ref, gv_ref, cond_hbm, zt_ref, yt_ref, xt_ref, out_ref,
-    cond_ref, masked, pieces, fields, gva, hots, phases,
+    own_ref, ve_ref, ce_ref, gv_ref, val_hbm, cond_hbm, zt_hbm, yt_hbm, xt_hbm, out_ref,
+    val_ref, cond_ref, zt_ref, yt_ref, xt_ref, masked, pieces, fields, gva, hots, phases,
     z_scr, y_scr, p_buf, c_rcv, s1, x_rcv, s2, z_rcv, t_buf, w_buf, r_ref, wo_ref, left, right,
-    load, ss, sr, gs, gr, vzs, vzr, vxs, vxr, vcs, vcr,
+    ready, load, ss, sr, gs, gr, vzs, vzr, vxs, vxr, vcs, vcr,
     cs, cr, xs, xr, zs, zr, ts, tr, ps, pr, xas, xar, cas, car,
 ):
     b = lax.axis_index("band")
@@ -99,39 +99,43 @@
     def greet(band, ga):
         pl.semaphore_signal(barrier, 1, device_id=(band, ga), device_id_type=MESH)
 
-    for s in range(4):
-        source = s * 8 + e
-
-        @pl.when(jnp.logical_or(source != b, a != b))
-        def _():
-            greet(source, b)
-
     for d in (2, 1, 3):
         greet(*at_z(lax.rem(zh + d, 4)))
         greet(*at_x(lax.rem(x + d, 4)))
     greet(b, other)
 
+    ys = [lax.rem(y + d, 8) for d in (4, 3, 5, 2, 6, 1, 7, 0)]
+
     def over_band(fn):
-        def step(i, carry):
-            u = lax.div(i, 4)
-            dy = 4 + (1 - 2 * lax.rem(u, 2)) * lax.div(u + 1, 2)
-            fn(lax.rem(zl + 1 + lax.rem(i, 4), 4) * 8 + lax.rem(y + dy, 8))
+        def step(d, carry):
+            base = lax.rem(zl + d, 4) * 8
+            for yy in ys:
+                fn(base + yy)
             return carry
 
-        lax.fori_loop(0, NB - 1, step, 0)
+        lax.fori_loop(1, 4, step, 0)
+        for yy in ys[:7]:
+            fn(zl * 8 + yy)
 
     over_band(lambda p: greet(p, a))
-    fetch = pltpu.make_async_copy(cond_hbm, cond_ref, load)
-    fetch.start()
+    sources = [val_hbm, cond_hbm, zt_hbm, yt_hbm, xt_hbm.at[a]]
+    places = [val_ref, cond_ref, zt_ref, yt_ref, xt_ref]
+    fetches = [
+        pltpu.make_async_copy(source, there, load.at[i])
+        for i, (source, there) in enumerate(zip(sources, places))
+    ]
+    for fetch in fetches:
+        fetch.start()
+    mine = c * 16 + x * 4 + zh
+    gva[mine] = gv_ref[...].reshape(1, NGD)
+    for xl in range(4):
+        y_scr[(xl * 16 + NF) * KB : (xl + 1) * 16 * KB, :] = jnp.zeros((4 * KB, 128), F32)
+    fetches[0].wait()
 
     for k in range(NV):
         flag = jnp.where(own_ref[k] == b, 1.0, 0.0).astype(F32)
         masked[k] = (val_ref[k].astype(F32) * flag).astype(BF16)
         pieces[k, b] = masked[k, b]
-    mine = c * 16 + x * 4 + zh
-    gva[mine] = gv_ref[...].reshape(1, NGD)
-    for xl in range(4):
-        y_scr[(xl * 16 + NF) * KB : (xl + 1) * 16 * KB, :] = jnp.zeros((4 * KB, 128), F32)
 
     x_order = [lax.rem(x + d, 4) for d in (2, 1, 3)]
     z_order = [lax.rem(zh + d, 4) for d in (2, 1, 3)] + [zh]
@@ -159,7 +163,7 @@
     def g_core(slot):
         return copy(gva.at[pl.ds(c * 16, 16)], gva.at[pl.ds(slot * 16, 16)], vcs, vcr, (b, other))
 
-    pl.semaphore_wait(barrier, 38 + 4 - jnp.where(a == b, 1, 0))
+    pl.semaphore_wait(barrier, 38)
     over_band(lambda p: piece(0, p).start())
     for zz in z_order[:3]:
         g_z(zz, zh).start()
@@ -182,7 +186,9 @@
     all_pieces(0).wait_send()
     all_pieces(1).wait_send()
 
-    xt = xt_ref[a]
+    for fetch in fetches[1:]:
+        fetch.wait()
+    xt = xt_ref[...]
     cell = lax.broadcasted_iota(jnp.int32, (128, NGD), 0)
     xcell = lax.broadcasted_iota(jnp.int32, (KB, NGD), 0)
 
@@ -196,13 +202,17 @@
 
     lax.fori_loop(c * 16, c * 16 + 16, prepare, 0)
     g_core(1 - c).wait_recv()
+
+    @pl.when(a == b)
+    def _():
+        over_band(lambda p: pl.semaphore_signal(ready, 1, device_id=(p, a), device_id_type=MESH))
+
     lax.fori_loop((1 - c) * 16, (1 - c) * 16 + 16, prepare, 0)
     for zz in z_order[:3]:
         g_z(zz, zh).wait_send()
     for xx in x_order:
         g_x(xx, x).wait_send()
     g_core(c).wait_send()
-    fetch.wait()
 
     low = lax.broadcasted_iota(jnp.int32, (1, 128), 1) < KB
     sign = jnp.where(low, -1.0, 1.0).astype(F32)
@@ -272,12 +282,13 @@
         p_buf[cc, zz, xx, 56:64, 64:128] = jnp.zeros((8, 64), F32)
 
     def select_group(zz):
-        def pair(xx, carry):
-            select(zz, xx, 1 - c)
-            select(zz, xx, c)
+        def pair(i, carry):
+            for xx in (2 * i, 2 * i + 1):
+                select(zz, xx, 1 - c)
+                select(zz, xx, c)
             return carry
 
-        lax.fori_loop(0, 4, pair, 0)
+        lax.fori_loop(0, 2, pair, 0)
 
     def to_core(zz):
         return copy(p_buf.at[1 - c, zz], c_rcv.at[zz], cs.at[zz], cr.at[zz], (b, other))
@@ -326,17 +337,17 @@
     total = (s2[zh] + z_rcv[z_order[0]]) + (z_rcv[z_order[1]] + z_rcv[z_order[2]])
     coeffs = total.astype(BF16)
     t_buf[...] = coeffs
+    @pl.when(a != b)
+    def _():
+        pl.semaphore_wait(ready, 1)
+
+    slot = lax.rem(y + 4, 8)
+
+    def to_rows(zz):
+        return copy(t_buf, r_ref.at[slot, zl], ts.at[zz], tr.at[zl], (a, zz * 8 + slot))
+
     for zz in z_order:
-        target = zz * 8 + y
-        stays = jnp.logical_and(a == b, target == a)
-
-        @pl.when(jnp.logical_not(stays))
-        def _():
-            copy(t_buf, r_ref.at[y, zl], ts.at[zz], tr.at[zl], (a, target)).start()
-
-        @pl.when(stays)
-        def _():
-            pltpu.make_async_copy(t_buf, r_ref.at[y, zl], tr.at[zl]).start()
+        to_rows(zz).start()
 
     weighted = coeffs.astype(F32)[0:24] * weights
     weighted = jnp.concatenate([weighted, jnp.zeros((8, PANEL), F32)], axis=0).astype(BF16)
@@ -374,7 +385,7 @@
     def place_weighted(base, ee):
         for s in range(4):
             at = (base + s) * 24
-            right[at : at + 24, :] = wo_ref[s * 8 + ee].astype(F32)[0:24]
+            right[at : at + 24, :] = wo_ref[s * 8 + lax.rem(ee + 4, 8)].astype(F32)[0:24]
 
     def product(half):
         rows = slice(half * 384, (half + 1) * 384)
@@ -386,7 +397,7 @@
         )
 
     for s in range(4):
-        pltpu.make_async_copy(t_buf, r_ref.at[e, s], tr.at[s]).wait()
+        copy(t_buf, r_ref.at[e, s], ts.at[s], tr.at[s], (b, other)).wait_recv()
         for xx in x_order:
             along_x(e, x, xx, s).start()
         along_core(e, s).start()
@@ -402,12 +413,7 @@
         place_weighted(4 * i, xx * 2 + c)
         place_weighted(16 + 4 * i, xx * 2 + 1 - c)
     for zz in z_order:
-        target = zz * 8 + y
-
-        @pl.when(jnp.logical_not(jnp.logical_and(a == b, target == a)))
-        def _():
-            copy(t_buf, r_ref.at[y, zl], ts.at[zz], tr.at[zl], (a, target)).wait_send()
-
+        to_rows(zz).wait_send()
     all_panels().wait_send()
     chi = product(0)
     for i, xx in enumerate([x] + x_order):
@@ -429,10 +435,14 @@
     return pl.pallas_call(
         main_kernel,
         out_shape=jax.ShapeDtypeStruct((NGD, PANEL), F32),
-        in_specs=[SMEM] * 3 + [VMEM] * 2 + [pl.BlockSpec(memory_space=pl.ANY)] + [VMEM] * 3,
+        in_specs=[SMEM] * 3 + [VMEM] + [pl.BlockSpec(memory_space=pl.ANY)] * 5,
         out_specs=VMEM,
         scratch_shapes=[
+            pltpu.VMEM(piece, BF16),
             pltpu.VMEM((NC, 4, NGRID, NGRID), BF16),
+            pltpu.VMEM(ztab.shape, BF16),
+            pltpu.VMEM(ytab.shape, BF16),
+            pltpu.VMEM(xtab.shape[1:], BF16),
             pltpu.VMEM(piece, BF16),
             pltpu.VMEM(piece, BF16),
             pltpu.VMEM(piece, BF16),
@@ -453,7 +463,8 @@
             pltpu.VMEM((NB, 32, PANEL), BF16),
             pltpu.VMEM((NB * 24, NGD), F32),
             pltpu.VMEM((NB * 24, PANEL), F32),
-            dma,
+            pltpu.SemaphoreType.REGULAR,
+            dma((5,)),
             dma((NV,)),
             dma((NV,)),
             dma((NV,)),
@@ -481,7 +492,7 @@
         ],
         compiler_params=pltpu.CompilerParams(collective_id=1, has_side_effects=True),
     )(
-        owners, val_energy, cond_energy, valence.reshape(piece), gvec_index, conduction, ztab, ytab, xtab
+        owners, val_energy, cond_energy, gvec_index, valence.reshape(piece), conduction, ztab, ytab, xtab
     )
 
 

time: 88.7 us -> 85.3 us (0.962)
  Pallas kernels: 86.9 us -> 83.5 us
    pallas_call x1, Pallas kernels: 86.9 us -> 83.5 us  [per_device(): pl.pallas_call(main_kernel, out_shape=jax.ShapeDtypeStruct((NGD, PANEL),...]
where the time goes in v4:
time: 85.3 us; the launch traced here: 85.1 us
  Pallas kernels  83.5 us (98%)
  local copies, waits for them, and re-layouts  1.59 us (2%)
    pallas_call x1, Pallas kernels, per_device(): pl.pallas_call(main_kernel, out_shape=jax.ShapeDtypeStruct((NGD, PANEL),...  83.5 us

profile of v4, /device:TPU:1, one launch (start us, length us, event | category | flops | bytes accessed | tf_op | source)
XLA Modules:
  0.0 85.1 jit_solution(1192686551281630068)
XLA Ops:
  0.0 83.5 %shard_map.91 = f32[320,128]{1,0:T(8,128)} custom-call(s32[2]{0:T(128)} %own_ref.1, f32[2]{0:T(128)} %ve_ref.1, f32[6]{0:T(128)} %ce_ref.1, s32[320]{0:T(512)} %gv_ref.1, bf16[2,32,16,128]{3,2,1,0:T(8,128)(2,1)} %bitcast.1, bf16[6,4,128,128]{3,2,1,0:T(8,128)(2,1)} %cond_hbm.1, bf16[256,256]{1,0:T(8,128)(2,1)} %constant.6.clone.zt_hbm, ...), custom_call_target="tpu_custom_call" | custom-call | tf_op jit(solution)/shard_map/pallas_call | solution.py:435
  83.5 1.6 %copy.11 = f32[320,128]{1,0:T(8,128)} copy(f32[320,128]{1,0:T(8,128)} %shard_map.91) | data formatting | bytes 327680

commit v5 on v4

--- a/solution.py
+++ b/solution.py
@@ -71,8 +71,8 @@
 
 
 def main_kernel(
-    own_ref, ve_ref, ce_ref, gv_ref, val_hbm, cond_hbm, zt_hbm, yt_hbm, xt_hbm, out_ref,
-    val_ref, cond_ref, zt_ref, yt_ref, xt_ref, masked, pieces, fields, gva, hots, phases,
+    own_hbm, ve_hbm, ce_hbm, gv_hbm, val_hbm, cond_hbm, zt_hbm, yt_hbm, xt_hbm, out_ref,
+    own_ref, gv_ref, val_ref, cond_ref, ve_ref, ce_ref, zt_ref, yt_ref, xt_ref, masked, pieces, fields, gva, hots, phases,
     z_scr, y_scr, p_buf, c_rcv, s1, x_rcv, s2, z_rcv, t_buf, w_buf, r_ref, wo_ref, left, right,
     ready, load, ss, sr, gs, gr, vzs, vzr, vxs, vxr, vcs, vcr,
     cs, cr, xs, xr, zs, zr, ts, tr, ps, pr, xas, xar, cas, car,
@@ -118,8 +118,8 @@
             fn(zl * 8 + yy)
 
     over_band(lambda p: greet(p, a))
-    sources = [val_hbm, cond_hbm, zt_hbm, yt_hbm, xt_hbm.at[a]]
-    places = [val_ref, cond_ref, zt_ref, yt_ref, xt_ref]
+    sources = [own_hbm, gv_hbm, val_hbm, cond_hbm, ve_hbm, ce_hbm, zt_hbm, yt_hbm, xt_hbm.at[a]]
+    places = [own_ref, gv_ref, val_ref, cond_ref, ve_ref, ce_ref, zt_ref, yt_ref, xt_ref]
     fetches = [
         pltpu.make_async_copy(source, there, load.at[i])
         for i, (source, there) in enumerate(zip(sources, places))
@@ -127,10 +127,10 @@
     for fetch in fetches:
         fetch.start()
     mine = c * 16 + x * 4 + zh
+    fetches[1].wait()
     gva[mine] = gv_ref[...].reshape(1, NGD)
-    for xl in range(4):
-        y_scr[(xl * 16 + NF) * KB : (xl + 1) * 16 * KB, :] = jnp.zeros((4 * KB, 128), F32)
     fetches[0].wait()
+    fetches[2].wait()
 
     for k in range(NV):
         flag = jnp.where(own_ref[k] == b, 1.0, 0.0).astype(F32)
@@ -186,7 +186,7 @@
     all_pieces(0).wait_send()
     all_pieces(1).wait_send()
 
-    for fetch in fetches[1:]:
+    for fetch in fetches[3:]:
         fetch.wait()
     xt = xt_ref[...]
     cell = lax.broadcasted_iota(jnp.int32, (128, NGD), 0)
@@ -197,7 +197,9 @@
         hots[j] = jnp.where(cell == (v & 127), 1.0, 0.0).astype(BF16)
         xhot = jnp.where(xcell == (v >> 7), 1.0, 0.0).astype(BF16)
         e3 = dot(xt, xhot)
-        phases[j] = e3[0:8] + (e3[8:16] + e3[16:24])
+        e8 = e3[0:8] + (e3[8:16] + e3[16:24])
+        for i in range(8):
+            phases[j, i * NF : (i + 1) * NF] = jnp.broadcast_to(e8[i : i + 1], (NF, NGD))
         return carry
 
     lax.fori_loop(c * 16, c * 16 + 16, prepare, 0)
@@ -235,7 +237,7 @@
             sums = both[:128] + both[128:]
             for i in range(2):
                 part = sums[:, i * 128 : (i + 1) * 128]
-                row = pl.multiple_of(((2 * pair + i) * 16 + f) * KB, KB)
+                row = pl.multiple_of(((2 * pair + i) * NF + f) * KB, KB)
                 y_scr[pl.ds(row, KB), :] = part[:KB] + pltpu.roll(part[KB:], KB, 1) * sign
 
     def field(f, carry):
@@ -252,29 +254,27 @@
     all_whole(0).wait_send()
     all_whole(1).wait_send()
 
-    lane = lax.broadcasted_iota(jnp.int32, (64, 128), 1) < KB
+    lane = lax.broadcasted_iota(jnp.int32, (4 * NF, 128), 1) < KB
 
     def select(zz, xx, cc):
         j = zz * 8 + xx * 2 + cc
-        y0 = y_scr[pl.ds(2 * j, 64, stride=KB), :]
-        y1 = y_scr[pl.ds(2 * j + 1, 64, stride=KB), :]
+        y0 = y_scr[pl.ds(2 * j, 4 * NF, stride=KB), :]
+        y1 = y_scr[pl.ds(2 * j + 1, 4 * NF, stride=KB), :]
         ur = jnp.where(lane, y0, pltpu.roll(y1, KB, 1))
         ui = jnp.where(lane, pltpu.roll(y0, KB, 1), y1)
         hl = jnp.concatenate(split(jnp.concatenate([ur, ui], axis=0)), axis=1)
         slot = cc * 16 + xx * 4 + zz
         hot = hots[slot]
         sel = dot(hl, jnp.concatenate([hot, hot], axis=0))
-        phase = phases[slot]
-        re = jnp.zeros((16, NGD), F32)
-        im = jnp.zeros((16, NGD), F32)
-        for xl in range(4):
-            sr = sel[xl * 16 : (xl + 1) * 16]
-            si = sel[64 + xl * 16 : 64 + (xl + 1) * 16]
-            er = phase[xl : xl + 1]
-            ei = phase[4 + xl : 5 + xl]
-            re = re + (sr * er - si * ei)
-            im = im + (si * er + sr * ei)
-        rows = jnp.concatenate([re[:NF], im[:NF]], axis=0)
+        sr, si = sel[: 4 * NF], sel[4 * NF :]
+        er, ei = phases[slot, : 4 * NF], phases[slot, 4 * NF :]
+        re = sr * er - si * ei
+        im = si * er + sr * ei
+        re = re[: 2 * NF] + re[2 * NF :]
+        im = im[: 2 * NF] + im[2 * NF :]
+        re = re[:NF] + re[NF:]
+        im = im[:NF] + im[NF:]
+        rows = jnp.concatenate([re, im], axis=0)
         p_buf[cc, zz, xx, 0:24] = rows[:, 0:128]
         p_buf[cc, zz, xx, 24:48] = rows[:, 128:256]
         p_buf[cc, zz, xx, 48:64, 0:64] = rows[0:16, 256:320]
@@ -434,12 +434,16 @@
     tile = (64, 128)
     return pl.pallas_call(
         main_kernel,
-        out_shape=jax.ShapeDtypeStruct((NGD, PANEL), F32),
-        in_specs=[SMEM] * 3 + [VMEM] + [pl.BlockSpec(memory_space=pl.ANY)] * 5,
+        out_shape=pltpu.VMEM((NGD, PANEL), F32),
+        in_specs=[pl.BlockSpec(memory_space=pl.ANY)] * 9,
         out_specs=VMEM,
         scratch_shapes=[
+            pltpu.SMEM((NV,), jnp.int32),
+            pltpu.VMEM((NGD,), jnp.int32),
             pltpu.VMEM(piece, BF16),
             pltpu.VMEM((NC, 4, NGRID, NGRID), BF16),
+            pltpu.SMEM((NV,), F32),
+            pltpu.SMEM((NC,), F32),
             pltpu.VMEM(ztab.shape, BF16),
             pltpu.VMEM(ytab.shape, BF16),
             pltpu.VMEM(xtab.shape[1:], BF16),
@@ -448,9 +452,9 @@
             pltpu.VMEM(piece, BF16),
             pltpu.VMEM((NGA, 1, NGD), jnp.int32),
             pltpu.VMEM((NGA, 128, NGD), BF16),
-            pltpu.VMEM((NGA, 8, NGD), F32),
+            pltpu.VMEM((NGA, 8 * NF, NGD), F32),
             pltpu.VMEM((2, 2 * NGRID, 2 * NGRID), BF16),
-            pltpu.VMEM((64 * KB, 128), F32),
+            pltpu.VMEM((4 * NF * KB, 128), F32),
             pltpu.VMEM((2, 4, 4) + tile, F32),
             pltpu.VMEM((4, 4) + tile, F32),
             pltpu.VMEM((4, 4) + tile, F32),
@@ -464,7 +468,7 @@
             pltpu.VMEM((NB * 24, NGD), F32),
             pltpu.VMEM((NB * 24, PANEL), F32),
             pltpu.SemaphoreType.REGULAR,
-            dma((5,)),
+            dma((9,)),
             dma((NV,)),
             dma((NV,)),
             dma((NV,)),

time: 85.3 us -> 82.4 us (0.966)
  Pallas kernels: 83.5 us -> 81.6 us
  local copies, waits for them, and re-layouts: 1.59 us -> 0.67 us
    pallas_call x1, Pallas kernels: 83.5 us -> 81.6 us  [per_device(): pl.pallas_call(main_kernel, out_shape=pltpu.VMEM((NGD, PANEL), F32), in_s...]
    unnamed x1, local copies, waits for them, and re-layouts: 1.59 us -> 0.67 us
where the time goes in v5:
time: 82.4 us; the launch traced here: 82.3 us
  Pallas kernels  81.6 us (99%)
    pallas_call x1, Pallas kernels, per_device(): pl.pallas_call(main_kernel, out_shape=pltpu.VMEM((NGD, PANEL), F32), in_s...  81.6 us

profile of v5, /device:TPU:1, one launch (start us, length us, event | category | flops | bytes accessed | tf_op | source)
XLA Modules:
  0.0 82.3 jit_solution(10131235174294067049)
XLA Ops:
  0.0 81.6 %shard_map.91 = f32[320,128]{1,0:T(8,128)S(1)} custom-call(s32[2]{0:T(128)} %own_hbm.1, f32[2]{0:T(128)} %ve_hbm.1, f32[6]{0:T(128)} %ce_hbm.1, s32[320]{0:T(512)} %gv_hbm.1, bf16[2,32,16,128]{3,2,1,0:T(8,128)(2,1)} %bitcast.1, bf16[6,4,128,128]{3,2,1,0:T(8,128)(2,1)} %cond_hbm.1, bf16[256,256]{1,0:T(8,128)(2,1)} %constant.6.clone.zt_hbm, ...), custom_call_target="tpu_custom_call" | custom-call | tf_op jit(solution)/shard_map/pallas_call | solution.py:435
  81.6 0.7 copy.11

commit v6 on v5

--- a/solution.py
+++ b/solution.py
@@ -219,7 +219,7 @@
     low = lax.broadcasted_iota(jnp.int32, (1, 128), 1) < KB
     sign = jnp.where(low, -1.0, 1.0).astype(F32)
 
-    def along_z(g):
+    def along_z(g, slot):
         wave = cond_ref[lax.rem(g, NC)].astype(F32).reshape(4 * NGRID, NGRID)
         pair = wave * fields[lax.div(g, NC)].astype(F32).reshape(4 * NGRID, NGRID)
         hl = jnp.concatenate(split(pair), axis=1)
@@ -227,30 +227,34 @@
         high, rest = split(both[:, :128] + both[:, 128:])
         for xl in range(4):
             rows = slice(xl * NGRID, (xl + 1) * NGRID)
-            z_scr[xl // 2, 0:NGRID, (xl % 2) * 128 : (xl % 2 + 1) * 128] = high[rows]
-            z_scr[xl // 2, NGRID : 2 * NGRID, (xl % 2) * 128 : (xl % 2 + 1) * 128] = rest[rows]
-
-    def along_y(g):
+            z_scr[slot, xl // 2, 0:NGRID, (xl % 2) * 128 : (xl % 2 + 1) * 128] = high[rows]
+            z_scr[slot, xl // 2, NGRID : 2 * NGRID, (xl % 2) * 128 : (xl % 2 + 1) * 128] = rest[rows]
+
+    def along_y(g, slot):
         f = lax.rem(g, NC) * NV + lax.div(g, NC)
         for pair in range(2):
-            both = dot(yt_ref[...], z_scr[pair])
+            both = dot(yt_ref[...], z_scr[slot, pair])
             sums = both[:128] + both[128:]
             for i in range(2):
                 part = sums[:, i * 128 : (i + 1) * 128]
                 row = pl.multiple_of(((2 * pair + i) * NF + f) * KB, KB)
                 y_scr[pl.ds(row, KB), :] = part[:KB] + pltpu.roll(part[KB:], KB, 1) * sign
 
-    def field(f, carry):
-        along_y(f - 1)
-        along_z(f)
-        return carry
+    def two_fields(i, g, first):
+        along_y(g - 1, 1 - first)
+        along_z(g, first)
+        along_y(g, first)
+        along_z(g + 1, 1 - first)
+        return i
 
     all_whole(0).wait_recv()
-    along_z(0)
-    lax.fori_loop(1, NC, field, 0)
+    along_z(0, 0)
+    lax.fori_loop(0, NC // 2 - 1, lambda i, n: two_fields(n, 2 * i + 1, 1), 0)
+    along_y(NC - 2, 0)
+    along_z(NC - 1, 1)
     all_whole(1).wait_recv()
-    lax.fori_loop(NC, NF, field, 0)
-    along_y(NF - 1)
+    lax.fori_loop(NC // 2, NC, lambda i, n: two_fields(n, 2 * i, 0), 0)
+    along_y(NF - 1, 1)
     all_whole(0).wait_send()
     all_whole(1).wait_send()
 
@@ -453,7 +457,7 @@
             pltpu.VMEM((NGA, 1, NGD), jnp.int32),
             pltpu.VMEM((NGA, 128, NGD), BF16),
             pltpu.VMEM((NGA, 8 * NF, NGD), F32),
-            pltpu.VMEM((2, 2 * NGRID, 2 * NGRID), BF16),
+            pltpu.VMEM((2, 2, 2 * NGRID, 2 * NGRID), BF16),
             pltpu.VMEM((4 * NF * KB, 128), F32),
             pltpu.VMEM((2, 4, 4) + tile, F32),
             pltpu.VMEM((4, 4) + tile, F32),

time: 82.4 us -> 81.8 us (level)
  no operation moved by 1% of the time
where the time goes in v6:
time: 81.8 us; the launch traced here: 81.6 us
  Pallas kernels  81 us (99%)
    pallas_call x1, Pallas kernels, per_device(): pl.pallas_call(main_kernel, out_shape=pltpu.VMEM((NGD, PANEL), F32), in_s...  81 us

profile of v6, /device:TPU:1, one launch (start us, length us, event | category | flops | bytes accessed | tf_op | source)
XLA Modules:
  0.0 81.6 jit_solution(13025082164215045827)
XLA Ops:
  0.0 81.0 %shard_map.91 = f32[320,128]{1,0:T(8,128)S(1)} custom-call(s32[2]{0:T(128)} %own_hbm.1, f32[2]{0:T(128)} %ve_hbm.1, f32[6]{0:T(128)} %ce_hbm.1, s32[320]{0:T(512)} %gv_hbm.1, bf16[2,32,16,128]{3,2,1,0:T(8,128)(2,1)} %bitcast.1, bf16[6,4,128,128]{3,2,1,0:T(8,128)(2,1)} %cond_hbm.1, bf16[256,256]{1,0:T(8,128)(2,1)} %constant.6.clone.zt_hbm, ...), custom_call_target="tpu_custom_call" | custom-call | tf_op jit(solution)/shard_map/pallas_call | solution.py:439
  81.0 0.7 copy.11
